TPU v7x, 256 devices: a whole 4x4x8 slice. The times are simulated.
256 devices in a mesh: rows: 16 (over z_hi, x, core), feat: 16 (over y, z_lo).
Axes of the slice: x: 4, y: 4, z: 8 (z_hi: 2, z_lo: 4; z = z_hi * 4 + z_lo), core: 2. Of those that a mesh axis runs over, the one named last changes fastest.
Arguments:
- design: bfloat16 [12288, 65536], P('rows', 'feat'), may hold values from -0.0234375 to 0.0234375
- labels: int32 [64, 12288], P(None, 'rows'), may hold values from -1 to 1, as said below
- local_x: float32 [16, 64, 65536], P('rows', None, 'feat'), may hold values from -6 to 6
- dual_u: float32 [16, 64, 65536], P('rows', None, 'feat'), may hold values from -3 to 3
- consensus_z: float32 [64, 65536], P(None, 'feat'), may hold values from -6 to 6
- step_size: float32 [64], replicated, may hold values from 0.5 to 1
- rho: float32 [64], replicated, may hold values from 0.5 to 1.5
- penalty: float32 [64], replicated, may hold values from 0.5 to 4
Outputs:
- new_x: float32 [16, 64, 65536], P('rows', None, 'feat')
- new_z: float32 [64, 65536], P(None, 'feat')
- new_u: float32 [16, 64, 65536], P('rows', None, 'feat')
Inputs may be any that keep to these rules, and one draw needn't show every extreme that they name: `labels`: each entry is -1 or 1.
All inputs are finite; a program needn't handle non-finite values.
Results may differ from a plain program's by a relative error of at most 0.0023.
Values may be sent and summed in bfloat16 or wider, within the bound.
A program may use at most 64 MiB of HBM per device.

v0:
```python
import jax
import jax.numpy as jnp
from jax import lax
from jax.sharding import PartitionSpec as P


def per_device(design, labels, local_x, dual_u, consensus_z, step_size, rho, penalty):
    x = local_x[0]
    dual = dual_u[0]
    sign = labels.astype(jnp.float32)
    eta = step_size[:, None]
    weight = rho[:, None]
    for turn in range(2):
        xb = x.astype(jnp.bfloat16)
        partial_margin = lax.dot_general(
            xb, design, (((1,), (1,)), ((), ())), preferred_element_type=jnp.float32
        )
        margin = lax.psum(partial_margin, "feat")
        resid = (sign * jax.nn.sigmoid(-sign * margin)).astype(jnp.bfloat16)
        grad = jnp.dot(resid, design, preferred_element_type=jnp.float32)
        x = x - eta * (weight * (x - consensus_z + dual) - grad)
    blocks_count = lax.axis_size("rows")
    limit = (penalty / (rho * blocks_count))[:, None]
    total = lax.psum(x + dual, "rows")
    mean = total / blocks_count
    new_z = mean - jnp.clip(mean, -limit, limit)
    new_u = dual + x - new_z
    return (x[None], new_z, new_u[None])


def solution(mesh):
    in_specs = (
        P("rows", "feat"),
        P(None, "rows"),
        P("rows", None, "feat"),
        P("rows", None, "feat"),
        P(None, "feat"),
        P(),
        P(),
        P(),
    )
    out_specs = (P("rows", None, "feat"), P(None, "feat"), P("rows", None, "feat"))
    return jax.shard_map(
        per_device, mesh=mesh, in_specs=in_specs, out_specs=out_specs, check_vma=False
    )
```

profile of v0, /device:TPU:1, one launch (start us, length us, event | category | flops | bytes accessed | tf_op | source)
XLA Modules:
  0.0 527.0 jit_solution(12647417744780522010)
XLA Ops:
  7.2 0.0 copy-start
  7.2 0.0 copy-start.4
  7.2 0.0 copy-start.5
  7.2 0.0 copy-start.1
  7.2 0.0 copy-start.3
  7.2 0.0 all-reduce.4.cloned.1.call-start
  7.3 6.0 %fusion.15 = f32[64,768]{1,0:T(8,128)} fusion(bf16[768,4096]{1,0:T(8,128)(2,1)} %param.8, f32[1,64,4096]{2,1,0:T(8,128)} %param.10), kind=kOutput, calls=%fused_computation.27 | convolution fusion | flops 402653184 | bytes 7536640 | tf_op jit(solution)/shard_map/dot_general | solution.py:15
  13.2 0.0 all-reduce.4.cloned.1.call-update
  13.2 0.0 all-reduce.6.cloned.1.call-start
  13.3 147.6 %all-reduce.4.cloned.1.call-done = f32[64,768]{1,0:T(8,128)} async-done(((f32[64,768]{1,0:T(8,128)}), f32[64,768]{1,0:T(8,128)}) %all-reduce.4.cloned.1.call-update) | async-done | bytes 196624 | tf_op jit(solution)/shard_map/psum | solution.py:18
  160.9 0.0 copy-done
  160.9 0.0 copy-done.4
  160.9 0.0 copy-done.5
  160.9 0.0 copy-done.1
  160.9 0.0 copy-done.3
  160.9 4.4 fusion.1
  165.3 0.0 copy-start.2
  165.4 5.6 %fusion.7 = f32[64,768]{1,0:T(8,128)} fusion(bf16[768,4096]{1,0:T(8,128)(2,1)} %param.8, f32[64,4096]{1,0:T(8,128)S(1)} %fusion.1), kind=kOutput, calls=%fused_computation.16 | convolution fusion | flops 402915328 | bytes 7536640 | tf_op jit(solution)/shard_map/dot_general | solution.py:15
  170.9 0.0 all-reduce.6.cloned.1.call-update
  171.0 0.0 copy-start.6
  171.0 0.0 all-reduce.8.cloned.1.call-start
  171.0 152.3 %all-reduce.6.cloned.1.call-done = f32[64,768]{1,0:T(8,128)} async-done(((f32[64,768]{1,0:T(8,128)}), f32[64,768]{1,0:T(8,128)}) %all-reduce.6.cloned.1.call-update) | async-done | bytes 196624 | tf_op jit(solution)/shard_map/psum | solution.py:18
  323.3 0.0 copy-done.2
  323.3 5.6 %bitcast_add_fusion = (f32[64,4096]{1,0:T(8,128)}, f32[64,4096]{1,0:T(8,128)}) fusion(f32[1,64,4096]{2,1,0:T(8,128)S(1)} %copy-done.1, f32[64,4096]{1,0:T(8,128)S(1)} %fusion.1, bf16[768,4096]{1,0:T(8,128)(2,1)} %param.8, f32[64,768]{1,0:T(8,128)} %all-reduce.6.cloned.1.call-done, s32[64,768]{1,0:T(8,128)S(1)} %copy-done.3, f32[64,4096]{1,0:T(8,128)S(1)} %copy-done.2, ...), kind=kOutput, calls=%fused_computation.6 | convolution fusion | flops 404881408 | bytes 11928064 | tf_op jit(solution)/shard_map/dot_general | solution.py:20
  328.9 0.0 all-reduce.8.cloned.1.call-update
  329.0 0.0 copy-done.6
  329.0 188.3 %all-reduce.8.cloned.1.call-done = f32[64,4096]{1,0:T(8,128)} async-done(((f32[64,4096]{1,0:T(8,128)}), f32[64,4096]{1,0:T(8,128)}) %all-reduce.8.cloned.1.call-update) | async-done | bytes 1048592 | tf_op jit(solution)/shard_map/psum | solution.py:24
  517.3 3.2 subtract_bitcast_fusion
  (1 shorter events, 0.0 us)
Async XLA Ops:
  7.2 153.8 %copy-start = (f32[1,64,4096]{2,1,0:T(8,128)S(1)}, f32[1,64,4096]{2,1,0:T(8,128)}, u32[]{:S(2)}) copy-start(f32[1,64,4096]{2,1,0:T(8,128)} %param.10) | copy-start | bytes 3145732
  7.2 153.7 %copy-start.4 = (f32[64]{0:T(128)S(1)}, f32[64]{0:T(128)}, u32[]{:S(2)}) copy-start(f32[64]{0:T(128)} %param.14) | copy-start | bytes 772
  7.2 153.7 %copy-start.5 = (f32[64]{0:T(128)S(1)}, f32[64]{0:T(128)}, u32[]{:S(2)}) copy-start(f32[64]{0:T(128)} %param.13) | copy-start | bytes 772
  7.2 153.7 %copy-start.1 = (f32[1,64,4096]{2,1,0:T(8,128)S(1)}, f32[1,64,4096]{2,1,0:T(8,128)}, u32[]{:S(2)}) copy-start(f32[1,64,4096]{2,1,0:T(8,128)} %param.11) | copy-start | bytes 3145732
  7.2 153.7 %copy-start.3 = (s32[64,768]{1,0:T(8,128)S(1)}, s32[64,768]{1,0:T(8,128)}, u32[]{:S(2)}) copy-start(s32[64,768]{1,0:T(8,128)} %param.9) | copy-start | bytes 589828
  7.2 153.7 %all-reduce.4.cloned.1.call-start = ((), (), s32[]{:S(2)}) async-start(), calls=%async_computation | async-start | bytes 393216 | tf_op jit(solution)/shard_map/psum | solution.py:18
  13.2 310.1 %all-reduce.6.cloned.1.call-start = ((), (), s32[]{:S(2)}) async-start(), calls=%async_computation.1 | async-start | bytes 393216 | tf_op jit(solution)/shard_map/psum | solution.py:18
  165.3 158.0 %copy-start.2 = (f32[64,4096]{1,0:T(8,128)S(1)}, f32[64,4096]{1,0:T(8,128)}, u32[]{:S(2)}) copy-start(f32[64,4096]{1,0:T(8,128)} %param.12) | copy-start | bytes 3145732
  171.0 158.0 %copy-start.6 = (f32[64]{0:T(128)S(1)}, f32[64]{0:T(128)}, u32[]{:S(2)}) copy-start(f32[64]{0:T(128)} %param.15) | copy-start | bytes 772
  171.0 346.3 %all-reduce.8.cloned.1.call-start = ((), (), s32[]{:S(2)}) async-start(), calls=%async_computation.2 | async-start | bytes 2097152 | tf_op jit(solution)/shard_map/psum | solution.py:24
Sparse Core Ops, SparseCore 0:
  13.4 147.5 all-reduce.3
  171.1 152.2 all-reduce.5
  329.1 188.1 all-reduce.7
where the time goes:
time: 527 us
  waiting for transfers between devices  488 us (93%)
  matrix products  21.5 us (4%)
  between operations  13.8 us (3%)
    psum x2, waiting for transfers between devices, per_device(): margin = lax.psum(partial_margin, 'feat')  300 us
    psum x1, waiting for transfers between devices, per_device(): total = lax.psum(x + dual, 'rows')  188 us
    dot_general x2, matrix products, per_device(): lax.dot_general(xb, design, (((1,), (1,)), ((), ())), preferred_element_t...  11.5 us
  transfers between devices with their start and end apart: 3, of which 3 were waited for; matrix products, arithmetic and copies ran while one was open for 0% of the time, Pallas kernels for 0%

commit v1 on v0

v1 whole, which is shorter than its diff:
```python
import functools

import jax
import jax.numpy as jnp
from jax import lax
from jax.experimental import pallas as pl
from jax.experimental.pallas import tpu as pltpu
from jax.sharding import PartitionSpec as P

MESH = pl.DeviceIdType.MESH
AXES = ("rows", "feat")


def _device(axis, peer):
    return tuple(peer if a == axis else lax.axis_index(a) for a in AXES)


def _allreduce_kernel(axis, n, x_ref, o_ref, recv, gath, ssem1, rsem1, ssem2, rsem2):
    me = lax.axis_index(axis)
    peers = [lax.rem(me + d, n) for d in range(n)]
    srcs = [lax.rem(me + n - d, n) for d in range(n)]

    barrier = pltpu.get_barrier_semaphore()
    for d in range(1, n):
        pl.semaphore_signal(barrier, inc=1, device_id=_device(axis, peers[d]), device_id_type=MESH)
    pl.semaphore_wait(barrier, n - 1)

    sends = []
    for d in range(1, n):
        c = pltpu.make_async_remote_copy(
            src_ref=x_ref.at[peers[d]],
            dst_ref=recv.at[me],
            send_sem=ssem1.at[d],
            recv_sem=rsem1.at[d],
            device_id=_device(axis, peers[d]),
            device_id_type=MESH,
        )
        c.start()
        sends.append(c)
    acc = x_ref[me]
    for d in range(1, n):
        pltpu.make_async_remote_copy(
            src_ref=x_ref.at[srcs[d]],
            dst_ref=recv.at[srcs[d]],
            send_sem=ssem1.at[d],
            recv_sem=rsem1.at[d],
            device_id=_device(axis, srcs[d]),
            device_id_type=MESH,
        ).wait_recv()
        acc = acc + recv[srcs[d]]
    gath[me] = acc

    sends2 = []
    for d in range(1, n):
        c = pltpu.make_async_remote_copy(
            src_ref=gath.at[me],
            dst_ref=gath.at[me],
            send_sem=ssem2.at[d],
            recv_sem=rsem2.at[d],
            device_id=_device(axis, peers[d]),
            device_id_type=MESH,
        )
        c.start()
        sends2.append(c)
    for c in sends:
        c.wait_send()
    for d in range(1, n):
        pltpu.make_async_remote_copy(
            src_ref=gath.at[srcs[d]],
            dst_ref=gath.at[srcs[d]],
            send_sem=ssem2.at[d],
            recv_sem=rsem2.at[d],
            device_id=_device(axis, srcs[d]),
            device_id_type=MESH,
        ).wait_recv()
    for c in sends2:
        c.wait_send()
    o_ref[...] = gath[...]


def allreduce(x, axis, n, cid):
    rows, width = x.shape
    chunk = rows // n
    xs = x.reshape(n, chunk, width)
    out = pl.pallas_call(
        functools.partial(_allreduce_kernel, axis, n),
        out_shape=jax.ShapeDtypeStruct(xs.shape, xs.dtype),
        in_specs=[pl.BlockSpec(memory_space=pltpu.VMEM)],
        out_specs=pl.BlockSpec(memory_space=pltpu.VMEM),
        scratch_shapes=[
            pltpu.VMEM(xs.shape, xs.dtype),
            pltpu.VMEM(xs.shape, xs.dtype),
            pltpu.SemaphoreType.DMA((n,)),
            pltpu.SemaphoreType.DMA((n,)),
            pltpu.SemaphoreType.DMA((n,)),
            pltpu.SemaphoreType.DMA((n,)),
        ],
        compiler_params=pltpu.CompilerParams(collective_id=cid, has_side_effects=True),
    )(xs)
    return out.reshape(rows, width)


def per_device(n_rows, n_feat, design, labels, local_x, dual_u, consensus_z, step_size, rho, penalty):
    x = local_x[0]
    dual = dual_u[0]
    sign = labels.astype(jnp.float32)
    eta = step_size[:, None]
    weight = rho[:, None]
    for turn in range(2):
        xb = x.astype(jnp.bfloat16)
        partial_margin = lax.dot_general(
            xb, design, (((1,), (1,)), ((), ())), preferred_element_type=jnp.float32
        )
        margin = allreduce(partial_margin, "feat", n_feat, 0)
        resid = (sign * jax.nn.sigmoid(-sign * margin)).astype(jnp.bfloat16)
        grad = jnp.dot(resid, design, preferred_element_type=jnp.float32)
        x = x - eta * (weight * (x - consensus_z + dual) - grad)
    limit = (penalty / (rho * n_rows))[:, None]
    total = allreduce(x + dual, "rows", n_rows, 1)
    mean = total / n_rows
    new_z = mean - jnp.clip(mean, -limit, limit)
    new_u = dual + x - new_z
    return (x[None], new_z, new_u[None])


def solution(mesh):
    in_specs = (
        P("rows", "feat"),
        P(None, "rows"),
        P("rows", None, "feat"),
        P("rows", None, "feat"),
        P(None, "feat"),
        P(),
        P(),
        P(),
    )
    out_specs = (P("rows", None, "feat"), P(None, "feat"), P("rows", None, "feat"))
    fn = functools.partial(per_device, mesh.shape["rows"], mesh.shape["feat"])
    return jax.shard_map(
        fn, mesh=mesh, in_specs=in_specs, out_specs=out_specs, check_vma=False
    )
```

time: 527 us -> 133 us (0.25)
  the two profiles are of different devices: /device:TPU:1 before, /device:TPU:15 now
where the time goes in v1:
time: 133 us
  Pallas kernels  103 us (77%)
  matrix products  17.7 us (13%)
  local copies, waits for them, and re-layouts  5.55 us (4%)
  other arithmetic  5.08 us (4%)
    pallas_call x3, Pallas kernels, allreduce(): pl.pallas_call(functools.partial(_allreduce_kernel, axis, n), out_shape=j...  103 us
    dot_general x2, matrix products, per_device(): grad = jnp.dot(resid, design, preferred_element_type=jnp.float32)  10.8 us
    dot_general x2, matrix products, per_device(): lax.dot_general(xb, design, (((1,), (1,)), ((), ())), preferred_element_t...  6.89 us

profile of v1, /device:TPU:15, one launch (start us, length us, event | category | flops | bytes accessed | tf_op | source)
XLA Modules:
  0.0 132.6 jit_solution(2314740020484139459)
XLA Ops:
  0.6 0.7 fusion.15
  1.3 1.3 convert_element_type.20
  2.6 0.2 convert_element_type.21
  2.8 0.0 copy-start
  2.8 0.0 copy-start.1
  2.8 0.0 copy-start.2
  2.8 4.9 %fusion = f32[16,4,768]{2,0,1:T(8,128)S(1)} fusion(bf16[768,4096]{1,0:T(8,128)(2,1)} %param.8, bf16[16,4,4096]{2,1,0:T(4,128)(2,1)S(1)} %convert_element_type.21), kind=kOutput, calls=%fused_computation | convolution fusion | flops 402653184 | bytes 7012352 | tf_op jit(solution)/shard_map/dot_general | solution.py:111
  7.7 0.8 copy.12.x_ref
  8.5 18.3 %shard_map.103 = f32[16,4,768]{2,1,0:T(4,128)} custom-call(f32[16,4,768]{2,1,0:T(4,128)} %copy.12.x_ref), custom_call_target="tpu_custom_call" | custom-call | tf_op jit(solution)/shard_map/pallas_call | solution.py:85
  26.8 0.0 slice-start
  26.8 1.1 reshape.30
  28.0 0.0 copy-done
  28.0 0.0 copy-done.1
  28.0 0.0 copy-done.2
  28.0 0.0 slice-start.1
  28.0 5.1 %fusion.3 = f32[64,4096]{1,0:T(8,128)S(1)} fusion(bf16[768,4096]{1,0:T(8,128)(2,1)} %param.8, f32[1,64,4096]{2,1,0:T(8,128)} %param.11, f32[1,64,4096]{2,1,0:T(8,128)} %param.10, f32[64,4096]{1,0:T(8,128)} %param.12, f32[64]{0:T(128)S(1)} %copy-done.1, f32[64]{0:T(128)S(1)} %copy-done.2, f32[64,768]{1,0:T(8,128)S(1)} %reshape.30, s32[64,768]{1,0:T(8,128)S(1)} %copy-done), kind=kOutput, calls=%fused_computation.5 | convolution fusion | flops 404619264 | bytes 10879488 | tf_op jit(solution)/shard_map/dot_general | solution.py:116
  33.1 0.0 slice-done
  33.1 0.0 slice-done.1
  33.1 2.0 %fusion.9 = f32[64,768]{1,0:T(8,128)S(1)} fusion(bf16[768,4096]{1,0:T(8,128)(2,1)S(1)} %bitcast.27, f32[64,4096]{1,0:T(8,128)S(1)} %fusion.3), kind=kOutput, calls=%fused_computation.18 | convolution fusion | flops 402915328 | bytes 7536640 | tf_op jit(solution)/shard_map/dot_general | solution.py:111
  35.1 0.7 reshape.31.x_ref
  35.9 15.6 %shard_map.104 = f32[16,4,768]{2,1,0:T(4,128)} custom-call(f32[16,4,768]{2,1,0:T(4,128)} %reshape.31.x_ref), custom_call_target="tpu_custom_call" | custom-call | tf_op jit(solution)/shard_map/pallas_call | solution.py:85
  51.5 1.0 reshape.32
  52.5 5.7 %bitcast_add_fusion = (f32[64,4096]{1,0:T(8,128)S(1)}, f32[64,4096]{1,0:T(8,128)}) fusion(f32[1,64,4096]{2,1,0:T(8,128)} %param.11, f32[64,4096]{1,0:T(8,128)S(1)} %fusion.3, bf16[768,4096]{1,0:T(8,128)(2,1)} %param.8, f32[64,768]{1,0:T(8,128)S(1)} %reshape.32, s32[64,768]{1,0:T(8,128)S(1)} %copy-done, f32[64,4096]{1,0:T(8,128)} %param.12, ...), kind=kOutput, calls=%fused_computation.8 | convolution fusion | flops 404881408 | bytes 11928064 | tf_op jit(solution)/shard_map/dot_general | solution.py:116
  58.2 1.3 reshape.33.x_ref
  59.5 69.6 %shard_map.105 = f32[16,4,4096]{2,1,0:T(4,128)} custom-call(f32[16,4,4096]{2,1,0:T(4,128)} %reshape.33.x_ref), custom_call_target="tpu_custom_call" | custom-call | tf_op jit(solution)/shard_map/pallas_call | solution.py:85
  129.1 1.5 %broadcast_multiply_fusion = f32[16,4,4096]{2,1,0:T(4,128)S(1)} fusion(f32[16,4,4096]{2,1,0:T(4,128)} %shard_map.105), kind=kLoop, calls=%fused_computation.17 | loop fusion | flops 262144 | bytes 2097152 | tf_op jit(solution)/shard_map/div | solution.py:120
  130.6 0.4 div.21
  131.0 1.6 %subtract_bitcast_fusion = (f32[1,64,4096]{2,1,0:T(8,128)}, f32[64,4096]{1,0:T(8,128)}) fusion(f32[64,4096]{1,0:T(8,128)S(1)} %get-tuple-element.7, f32[64,4096]{1,0:T(8,128)S(1)} %div.21, f32[64]{0:T(128)S(1)} %get-tuple-element.5, f32[64]{0:T(128)S(1)} %get-tuple-element.6), kind=kLoop, calls=%fused_computation.14 | loop fusion | flops 1048576 | bytes 4194816 | tf_op jit(solution)/shard_map/broadcast_in_dim | solution.py:123
  (1 shorter events, 0.0 us)
Async XLA Ops:
  2.8 25.2 %copy-start = (s32[64,768]{1,0:T(8,128)S(1)}, s32[64,768]{1,0:T(8,128)}, u32[]{:S(2)}) copy-start(s32[64,768]{1,0:T(8,128)} %param.9) | copy-start | bytes 589828
  2.8 25.2 %copy-start.1 = (f32[64]{0:T(128)S(1)}, f32[64]{0:T(128)}, u32[]{:S(2)}) copy-start(f32[64]{0:T(128)} %param.14) | copy-start | bytes 772
  2.8 25.2 %copy-start.2 = (f32[64]{0:T(128)S(1)}, f32[64]{0:T(128)}, u32[]{:S(2)}) copy-start(f32[64]{0:T(128)} %param.13) | copy-start | bytes 772
  26.8 6.3 %slice-start = ((s8[6291456]{0:T(1024)(128)(4,1)}), s8[2097152]{0:T(1024)(128)(4,1)S(1)}, s32[]{:S(2)}) async-start(s8[6291456]{0:T(1024)(128)(4,1)} %bitcast.26), calls=%async_computation | async-start | bytes 4194304
  28.0 5.1 %slice-start.1 = ((s8[6291456]{0:T(1024)(128)(4,1)}), s8[4194304]{0:T(1024)(128)(4,1)S(1)}, s32[]{:S(2)}) async-start(s8[6291456]{0:T(1024)(128)(4,1)} %bitcast.26), calls=%async_computation.1 | async-start | bytes 8388608

commit v2 on v1

--- a/solution.py
+++ b/solution.py
@@ -15,10 +15,16 @@
     return tuple(peer if a == axis else lax.axis_index(a) for a in AXES)
 
 
-def _allreduce_kernel(axis, n, x_ref, o_ref, recv, gath, ssem1, rsem1, ssem2, rsem2):
+def _allreduce_kernel(axis, n, rh, cw, x_ref, o_ref, recv, gath, ssem1, rsem1, ssem2, rsem2):
     me = lax.axis_index(axis)
     peers = [lax.rem(me + d, n) for d in range(n)]
     srcs = [lax.rem(me + n - d, n) for d in range(n)]
+    cblocks = x_ref.shape[1] // cw
+
+    def block(ref, p):
+        r = pl.multiple_of((p // cblocks) * rh, 8)
+        c = pl.multiple_of((p % cblocks) * cw, 128)
+        return ref.at[pl.ds(r, rh), pl.ds(c, cw)]
 
     barrier = pltpu.get_barrier_semaphore()
     for d in range(1, n):
@@ -28,7 +34,7 @@
     sends = []
     for d in range(1, n):
         c = pltpu.make_async_remote_copy(
-            src_ref=x_ref.at[peers[d]],
+            src_ref=block(x_ref, peers[d]),
             dst_ref=recv.at[me],
             send_sem=ssem1.at[d],
             recv_sem=rsem1.at[d],
@@ -37,10 +43,10 @@
         )
         c.start()
         sends.append(c)
-    acc = x_ref[me]
+    acc = block(x_ref, me)[...]
     for d in range(1, n):
         pltpu.make_async_remote_copy(
-            src_ref=x_ref.at[srcs[d]],
+            src_ref=recv.at[srcs[d]],
             dst_ref=recv.at[srcs[d]],
             send_sem=ssem1.at[d],
             recv_sem=rsem1.at[d],
@@ -75,29 +81,30 @@
         ).wait_recv()
     for c in sends2:
         c.wait_send()
-    o_ref[...] = gath[...]
+    for p in range(n):
+        r, c = (p // cblocks) * rh, (p % cblocks) * cw
+        o_ref[r:r + rh, c:c + cw] = gath[p]
 
 
 def allreduce(x, axis, n, cid):
     rows, width = x.shape
-    chunk = rows // n
-    xs = x.reshape(n, chunk, width)
-    out = pl.pallas_call(
-        functools.partial(_allreduce_kernel, axis, n),
-        out_shape=jax.ShapeDtypeStruct(xs.shape, xs.dtype),
+    rblocks = min(rows // 8, n)
+    rh, cw = rows // rblocks, width * rblocks // n
+    return pl.pallas_call(
+        functools.partial(_allreduce_kernel, axis, n, rh, cw),
+        out_shape=jax.ShapeDtypeStruct(x.shape, x.dtype),
         in_specs=[pl.BlockSpec(memory_space=pltpu.VMEM)],
         out_specs=pl.BlockSpec(memory_space=pltpu.VMEM),
         scratch_shapes=[
-            pltpu.VMEM(xs.shape, xs.dtype),
-            pltpu.VMEM(xs.shape, xs.dtype),
+            pltpu.VMEM((n, rh, cw), x.dtype),
+            pltpu.VMEM((n, rh, cw), x.dtype),
             pltpu.SemaphoreType.DMA((n,)),
             pltpu.SemaphoreType.DMA((n,)),
             pltpu.SemaphoreType.DMA((n,)),
             pltpu.SemaphoreType.DMA((n,)),
         ],
         compiler_params=pltpu.CompilerParams(collective_id=cid, has_side_effects=True),
-    )(xs)
-    return out.reshape(rows, width)
+    )(x)
 
 
 def per_device(n_rows, n_feat, design, labels, local_x, dual_u, consensus_z, step_size, rho, penalty):

time: 133 us -> 129 us (0.970)
  the two profiles are of different devices: /device:TPU:15 before, /device:TPU:7 now
where the time goes in v2:
time: 129 us
  Pallas kernels  104 us (81%)
  matrix products  19.8 us (15%)
  other arithmetic  3.91 us (3%)
    pallas_call x3, Pallas kernels, allreduce(): pl.pallas_call(functools.partial(_allreduce_kernel, axis, n, rh, cw), out...  104 us
    dot_general x2, matrix products, per_device(): grad = jnp.dot(resid, design, preferred_element_type=jnp.float32)  11.3 us
    dot_general x2, matrix products, per_device(): lax.dot_general(xb, design, (((1,), (1,)), ((), ())), preferred_element_t...  8.53 us
    broadcast_in_dim x1, other arithmetic, per_device(): return (x[None], new_z, new_u[None])  3.19 us

profile of v2, /device:TPU:7, one launch (start us, length us, event | category | flops | bytes accessed | tf_op | source)
XLA Modules:
  0.0 128.8 jit_solution(11735028761236625487)
XLA Ops:
  0.6 0.0 copy-start.1
  0.6 0.0 copy-start.2
  0.7 0.0 copy-start
  0.7 0.7 fusion.14
  1.4 5.8 %fusion.15.x_ref = f32[64,768]{1,0:T(8,128)} fusion(bf16[768,4096]{1,0:T(8,128)(2,1)} %param.8, f32[1,64,4096]{2,1,0:T(8,128)} %param.10), kind=kOutput, calls=%fused_computation.27 | convolution fusion | flops 402653184 | bytes 7536640 | tf_op jit(solution)/shard_map/dot_general | solution.py:118
  7.2 0.0 slice-start
  7.2 18.9 %shard_map.103 = f32[64,768]{1,0:T(8,128)} custom-call(f32[64,768]{1,0:T(8,128)} %fusion.15.x_ref), custom_call_target="tpu_custom_call" | custom-call | tf_op jit(solution)/shard_map/pallas_call | solution.py:93
  26.1 0.0 copy-done.1
  26.1 0.0 copy-done.2
  26.2 0.0 copy-done
  26.2 0.0 slice-start.1
  26.2 5.1 %fusion.1 = f32[64,4096]{1,0:T(8,128)S(1)} fusion(bf16[768,4096]{1,0:T(8,128)(2,1)} %param.8, f32[1,64,4096]{2,1,0:T(8,128)} %param.11, f32[1,64,4096]{2,1,0:T(8,128)} %param.10, f32[64,4096]{1,0:T(8,128)} %param.12, f32[64]{0:T(128)S(1)} %copy-done.1, f32[64]{0:T(128)S(1)} %copy-done.2, f32[64,768]{1,0:T(8,128)} %shard_map.103, s32[64,768]{1,0:T(8,128)S(1)} %copy-done), kind=kOutput, calls=%fused_computation.3 | convolution fusion | flops 404619264 | bytes 10879488 | tf_op jit(solution)/shard_map/dot_general | solution.py:123
  31.3 0.0 slice-done
  31.3 0.0 slice-done.1
  31.4 2.7 %fusion.7.x_ref = f32[64,768]{1,0:T(8,128)} fusion(bf16[768,4096]{1,0:T(8,128)(2,1)S(1)} %bitcast.36, f32[64,4096]{1,0:T(8,128)S(1)} %fusion.1), kind=kOutput, calls=%fused_computation.16 | convolution fusion | flops 402915328 | bytes 7536640 | tf_op jit(solution)/shard_map/dot_general | solution.py:118
  34.1 15.8 %shard_map.104 = f32[64,768]{1,0:T(8,128)} custom-call(f32[64,768]{1,0:T(8,128)} %fusion.7.x_ref), custom_call_target="tpu_custom_call" | custom-call | tf_op jit(solution)/shard_map/pallas_call | solution.py:93
  49.8 6.1 %bitcast_add_fusion = (f32[64,4096]{1,0:T(8,128)}, f32[64,4096]{1,0:T(8,128)}) fusion(f32[1,64,4096]{2,1,0:T(8,128)} %param.11, f32[64,4096]{1,0:T(8,128)S(1)} %fusion.1, bf16[768,4096]{1,0:T(8,128)(2,1)} %param.8, f32[64,768]{1,0:T(8,128)} %shard_map.104, s32[64,768]{1,0:T(8,128)S(1)} %copy-done, f32[64,4096]{1,0:T(8,128)} %param.12, f32[64]{0:T(128)S(1)} %copy-done.1, ...), kind=kOutput, calls=%fused_computation.6 | convolution fusion | flops 404881408 | bytes 11928064 | tf_op jit(solution)/shard_map/dot_general | solution.py:123
  55.9 69.7 %shard_map.105 = f32[64,4096]{1,0:T(8,128)} custom-call(f32[64,4096]{1,0:T(8,128)} %get-tuple-element.7.x_ref), custom_call_target="tpu_custom_call" | custom-call | tf_op jit(solution)/shard_map/pallas_call | solution.py:93
  125.7 3.2 %subtract_bitcast_fusion = (f32[1,64,4096]{2,1,0:T(8,128)}, f32[64,4096]{1,0:T(8,128)}) fusion(f32[64,4096]{1,0:T(8,128)} %get-tuple-element.7.x_ref, f32[64]{0:T(128)S(1)} %get-tuple-element.5, f32[64]{0:T(128)S(1)} %get-tuple-element.6, f32[64,4096]{1,0:T(8,128)} %shard_map.105), kind=kLoop, calls=%fused_computation.13 | loop fusion | flops 1310720 | bytes 4194816 | tf_op jit(solution)/shard_map/broadcast_in_dim | solution.py:130
  (1 shorter events, 0.0 us)
Async XLA Ops:
  0.6 25.5 %copy-start.1 = (f32[64]{0:T(128)S(1)}, f32[64]{0:T(128)}, u32[]{:S(2)}) copy-start(f32[64]{0:T(128)} %param.14) | copy-start | bytes 772
  0.6 25.5 %copy-start.2 = (f32[64]{0:T(128)S(1)}, f32[64]{0:T(128)}, u32[]{:S(2)}) copy-start(f32[64]{0:T(128)} %param.13) | copy-start | bytes 772
  0.7 25.5 %copy-start = (s32[64,768]{1,0:T(8,128)S(1)}, s32[64,768]{1,0:T(8,128)}, u32[]{:S(2)}) copy-start(s32[64,768]{1,0:T(8,128)} %param.9) | copy-start | bytes 589828
  7.2 24.1 %slice-start = ((s8[6291456]{0:T(1024)(128)(4,1)}), s8[2097152]{0:T(1024)(128)(4,1)S(1)}, s32[]{:S(2)}) async-start(s8[6291456]{0:T(1024)(128)(4,1)} %bitcast.35), calls=%async_computation | async-start | bytes 4194304
  26.2 5.2 %slice-start.1 = ((s8[6291456]{0:T(1024)(128)(4,1)}), s8[4194304]{0:T(1024)(128)(4,1)S(1)}, s32[]{:S(2)}) async-start(s8[6291456]{0:T(1024)(128)(4,1)} %bitcast.35), calls=%async_computation.1 | async-start | bytes 8388608

commit v3 on v2

--- a/solution.py
+++ b/solution.py
@@ -87,6 +87,8 @@
 
 
 def allreduce(x, axis, n, cid):
+    if n == 1:
+        return x
     rows, width = x.shape
     rblocks = min(rows // 8, n)
     rh, cw = rows // rblocks, width * rblocks // n
@@ -102,6 +104,101 @@
             pltpu.SemaphoreType.DMA((n,)),
             pltpu.SemaphoreType.DMA((n,)),
             pltpu.SemaphoreType.DMA((n,)),
+        ],
+        compiler_params=pltpu.CompilerParams(collective_id=cid, has_side_effects=True),
+    )(x)
+
+
+def _rows_kernel(nx, x_ref, o_ref, ra, hbuf, rb, rc, gb, ge,
+                 ssa, rsa, ssb, rsb, ssc, rsc, ssd, rsd, sse, rse):
+    r = lax.axis_index("rows")
+    n = 4 * nx
+    half, blk = x_ref.shape[0] // 2, x_ref.shape[0] // (2 * nx)
+    c = lax.rem(r, 2)
+    xi = lax.rem(r // 2, nx)
+    base = r - 2 * xi
+    partner = r + 1 - 2 * c
+    xpeers = [base + 2 * lax.rem(xi + d, nx) for d in range(nx)]
+    xsrcs = [lax.rem(xi + nx - d, nx) for d in range(nx)]
+    zpeer = lax.rem(r + 2 * nx, n)
+
+    def dev(p):
+        return _device("rows", p)
+
+    def rcopy(src, dst, ss, rs, p):
+        return pltpu.make_async_remote_copy(
+            src_ref=src, dst_ref=dst, send_sem=ss, recv_sem=rs,
+            device_id=dev(p), device_id_type=MESH)
+
+    barrier = pltpu.get_barrier_semaphore()
+    for p in [partner, zpeer] + xpeers[1:]:
+        pl.semaphore_signal(barrier, inc=1, device_id=dev(p), device_id_type=MESH)
+    pl.semaphore_wait(barrier, nx + 1)
+
+    mine = pl.multiple_of(c * half, 8)
+    other = pl.multiple_of((1 - c) * half, 8)
+    a = rcopy(x_ref.at[pl.ds(other, half)], ra, ssa, rsa, partner)
+    a.start()
+    a.wait()
+    hbuf[...] = x_ref[pl.ds(mine, half), :] + ra[...]
+
+    bs = []
+    for d in range(1, nx):
+        j = lax.rem(xi + d, nx)
+        cp = rcopy(hbuf.at[pl.ds(pl.multiple_of(j * blk, 8), blk)], rb.at[xi],
+                   ssb.at[d], rsb.at[d], xpeers[d])
+        cp.start()
+        bs.append(cp)
+    acc = hbuf[pl.ds(pl.multiple_of(xi * blk, 8), blk), :]
+    for d in range(1, nx):
+        rcopy(rb.at[xsrcs[d]], rb.at[xsrcs[d]], ssb.at[d], rsb.at[d], xpeers[d]).wait_recv()
+        acc = acc + rb[xsrcs[d]]
+    gb[xi] = acc
+
+    cz = rcopy(gb.at[xi], rc, ssc, rsc, zpeer)
+    cz.start()
+    cz.wait()
+    gb[xi] = gb[xi] + rc[...]
+
+    ds_ = []
+    for d in range(1, nx):
+        cp = rcopy(gb.at[xi], gb.at[xi], ssd.at[d], rsd.at[d], xpeers[d])
+        cp.start()
+        ds_.append(cp)
+    for cp in bs:
+        cp.wait_send()
+    for d in range(1, nx):
+        rcopy(gb.at[xsrcs[d]], gb.at[xsrcs[d]], ssd.at[d], rsd.at[d], xpeers[d]).wait_recv()
+    for cp in ds_:
+        cp.wait_send()
+
+    e = rcopy(gb, ge, sse, rse, partner)
+    e.start()
+    e.wait()
+    for j in range(nx):
+        o_ref[pl.ds(pl.multiple_of(mine + j * blk, 8), blk), :] = gb[j]
+        o_ref[pl.ds(pl.multiple_of(other + j * blk, 8), blk), :] = ge[j]
+
+
+def rows_allreduce(x, n, cid):
+    rows, width = x.shape
+    nx = n // 4
+    half, blk = rows // 2, rows // (2 * nx)
+    dma = pltpu.SemaphoreType.DMA
+    return pl.pallas_call(
+        functools.partial(_rows_kernel, nx),
+        out_shape=jax.ShapeDtypeStruct(x.shape, x.dtype),
+        in_specs=[pl.BlockSpec(memory_space=pltpu.VMEM)],
+        out_specs=pl.BlockSpec(memory_space=pltpu.VMEM),
+        scratch_shapes=[
+            pltpu.VMEM((half, width), x.dtype),
+            pltpu.VMEM((half, width), x.dtype),
+            pltpu.VMEM((nx, blk, width), x.dtype),
+            pltpu.VMEM((blk, width), x.dtype),
+            pltpu.VMEM((nx, blk, width), x.dtype),
+            pltpu.VMEM((nx, blk, width), x.dtype),
+            dma(()), dma(()), dma((nx,)), dma((nx,)), dma(()), dma(()),
+            dma((nx,)), dma((nx,)), dma(()), dma(()),
         ],
         compiler_params=pltpu.CompilerParams(collective_id=cid, has_side_effects=True),
     )(x)
@@ -123,7 +220,7 @@
         grad = jnp.dot(resid, design, preferred_element_type=jnp.float32)
         x = x - eta * (weight * (x - consensus_z + dual) - grad)
     limit = (penalty / (rho * n_rows))[:, None]
-    total = allreduce(x + dual, "rows", n_rows, 1)
+    total = rows_allreduce(x + dual, n_rows, 1)
     mean = total / n_rows
     new_z = mean - jnp.clip(mean, -limit, limit)
     new_u = dual + x - new_z

time: 129 us -> 100 us (0.78)
  the two profiles are of different devices: /device:TPU:7 before, /device:TPU:1 now
where the time goes in v3:
time: 100 us; the launch traced here: 99.9 us
  Pallas kernels  75.4 us (75%)
  matrix products  19.8 us (20%)
  other arithmetic  3.91 us (4%)
    pallas_call x1, Pallas kernels, rows_allreduce(): pl.pallas_call(functools.partial(_rows_kernel, nx), out_shape=jax.ShapeDt...  40 us
    pallas_call x2, Pallas kernels, allreduce(): pl.pallas_call(functools.partial(_allreduce_kernel, axis, n, rh, cw), out...  35.5 us
    dot_general x2, matrix products, per_device(): grad = jnp.dot(resid, design, preferred_element_type=jnp.float32)  11.3 us
    dot_general x2, matrix products, per_device(): lax.dot_general(xb, design, (((1,), (1,)), ((), ())), preferred_element_t...  8.54 us
    broadcast_in_dim x1, other arithmetic, per_device(): return (x[None], new_z, new_u[None])  3.19 us

profile of v3, /device:TPU:1, one launch (start us, length us, event | category | flops | bytes accessed | tf_op | source)
XLA Modules:
  0.0 99.9 jit_solution(8006722057022996174)
XLA Ops:
  0.6 0.0 copy-start.1
  0.6 0.0 copy-start.2
  0.7 0.0 copy-start
  0.7 0.7 fusion.14
  1.4 5.8 %fusion.15.x_ref = f32[64,768]{1,0:T(8,128)} fusion(bf16[768,4096]{1,0:T(8,128)(2,1)} %param.8, f32[1,64,4096]{2,1,0:T(8,128)} %param.10), kind=kOutput, calls=%fused_computation.27 | convolution fusion | flops 402653184 | bytes 7536640 | tf_op jit(solution)/shard_map/dot_general | solution.py:215
  7.2 0.0 slice-start
  7.2 19.7 %shard_map.103 = f32[64,768]{1,0:T(8,128)} custom-call(f32[64,768]{1,0:T(8,128)} %fusion.15.x_ref), custom_call_target="tpu_custom_call" | custom-call | tf_op jit(solution)/shard_map/pallas_call | solution.py:95
  27.0 0.0 copy-done.1
  27.0 0.0 copy-done.2
  27.0 0.0 copy-done
  27.0 0.0 slice-start.1
  27.0 5.1 %fusion.1 = f32[64,4096]{1,0:T(8,128)S(1)} fusion(bf16[768,4096]{1,0:T(8,128)(2,1)} %param.8, f32[1,64,4096]{2,1,0:T(8,128)} %param.11, f32[1,64,4096]{2,1,0:T(8,128)} %param.10, f32[64,4096]{1,0:T(8,128)} %param.12, f32[64]{0:T(128)S(1)} %copy-done.1, f32[64]{0:T(128)S(1)} %copy-done.2, f32[64,768]{1,0:T(8,128)} %shard_map.103, s32[64,768]{1,0:T(8,128)S(1)} %copy-done), kind=kOutput, calls=%fused_computation.3 | convolution fusion | flops 404619264 | bytes 10879488 | tf_op jit(solution)/shard_map/dot_general | solution.py:220
  32.2 0.0 slice-done
  32.2 0.0 slice-done.1
  32.2 2.7 %fusion.7.x_ref = f32[64,768]{1,0:T(8,128)} fusion(bf16[768,4096]{1,0:T(8,128)(2,1)S(1)} %bitcast.36, f32[64,4096]{1,0:T(8,128)S(1)} %fusion.1), kind=kOutput, calls=%fused_computation.16 | convolution fusion | flops 402915328 | bytes 7536640 | tf_op jit(solution)/shard_map/dot_general | solution.py:215
  34.9 15.7 %shard_map.104 = f32[64,768]{1,0:T(8,128)} custom-call(f32[64,768]{1,0:T(8,128)} %fusion.7.x_ref), custom_call_target="tpu_custom_call" | custom-call | tf_op jit(solution)/shard_map/pallas_call | solution.py:95
  50.6 6.1 %bitcast_add_fusion = (f32[64,4096]{1,0:T(8,128)}, f32[64,4096]{1,0:T(8,128)}) fusion(f32[1,64,4096]{2,1,0:T(8,128)} %param.11, f32[64,4096]{1,0:T(8,128)S(1)} %fusion.1, bf16[768,4096]{1,0:T(8,128)(2,1)} %param.8, f32[64,768]{1,0:T(8,128)} %shard_map.104, s32[64,768]{1,0:T(8,128)S(1)} %copy-done, f32[64,4096]{1,0:T(8,128)} %param.12, f32[64]{0:T(128)S(1)} %copy-done.1, ...), kind=kOutput, calls=%fused_computation.6 | convolution fusion | flops 404881408 | bytes 11928064 | tf_op jit(solution)/shard_map/dot_general | solution.py:220
  56.8 40.0 %shard_map.105 = f32[64,4096]{1,0:T(8,128)} custom-call(f32[64,4096]{1,0:T(8,128)} %get-tuple-element.7.x_ref), custom_call_target="tpu_custom_call" | custom-call | tf_op jit(solution)/shard_map/pallas_call | solution.py:188
  96.7 3.2 %subtract_bitcast_fusion = (f32[1,64,4096]{2,1,0:T(8,128)}, f32[64,4096]{1,0:T(8,128)}) fusion(f32[64,4096]{1,0:T(8,128)} %get-tuple-element.7.x_ref, f32[64]{0:T(128)S(1)} %get-tuple-element.5, f32[64]{0:T(128)S(1)} %get-tuple-element.6, f32[64,4096]{1,0:T(8,128)} %shard_map.105), kind=kLoop, calls=%fused_computation.13 | loop fusion | flops 1310720 | bytes 4194816 | tf_op jit(solution)/shard_map/broadcast_in_dim | solution.py:227
  (1 shorter events, 0.0 us)
Async XLA Ops:
  0.6 26.3 %copy-start.1 = (f32[64]{0:T(128)S(1)}, f32[64]{0:T(128)}, u32[]{:S(2)}) copy-start(f32[64]{0:T(128)} %param.14) | copy-start | bytes 772
  0.6 26.3 %copy-start.2 = (f32[64]{0:T(128)S(1)}, f32[64]{0:T(128)}, u32[]{:S(2)}) copy-start(f32[64]{0:T(128)} %param.13) | copy-start | bytes 772
  0.7 26.3 %copy-start = (s32[64,768]{1,0:T(8,128)S(1)}, s32[64,768]{1,0:T(8,128)}, u32[]{:S(2)}) copy-start(s32[64,768]{1,0:T(8,128)} %param.9) | copy-start | bytes 589828
  7.2 24.9 %slice-start = ((s8[6291456]{0:T(1024)(128)(4,1)}), s8[2097152]{0:T(1024)(128)(4,1)S(1)}, s32[]{:S(2)}) async-start(s8[6291456]{0:T(1024)(128)(4,1)} %bitcast.35), calls=%async_computation | async-start | bytes 4194304
  27.0 5.2 %slice-start.1 = ((s8[6291456]{0:T(1024)(128)(4,1)}), s8[4194304]{0:T(1024)(128)(4,1)S(1)}, s32[]{:S(2)}) async-start(s8[6291456]{0:T(1024)(128)(4,1)} %bitcast.35), calls=%async_computation.1 | async-start | bytes 8388608

commit v4 on v3

v4 whole, which is shorter than its diff:
```python
import functools

import jax
import jax.numpy as jnp
from jax import lax
from jax.experimental import pallas as pl
from jax.experimental.pallas import tpu as pltpu
from jax.sharding import PartitionSpec as P

MESH = pl.DeviceIdType.MESH
AXES = ("rows", "feat")
TILE = 512


def _device(axis, peer):
    return tuple(peer if a == axis else lax.axis_index(a) for a in AXES)


def _rcopy(axis, src, dst, ss, rs, p):
    return pltpu.make_async_remote_copy(
        src_ref=src, dst_ref=dst, send_sem=ss, recv_sem=rs,
        device_id=_device(axis, p), device_id_type=MESH)


def _feat_allreduce(n, rh, cw, x_ref, o_ref, recv, gath, ss1, rs1, ss2, rs2):
    me = lax.axis_index("feat")
    peers = [lax.rem(me + d, n) for d in range(n)]
    srcs = [lax.rem(me + n - d, n) for d in range(n)]
    cblocks = x_ref.shape[1] // cw

    def block(ref, p):
        r = pl.multiple_of((p // cblocks) * rh, 8)
        c = pl.multiple_of((p % cblocks) * cw, 128)
        return ref.at[pl.ds(r, rh), pl.ds(c, cw)]

    sends = []
    for d in range(1, n):
        c = _rcopy("feat", block(x_ref, peers[d]), recv.at[me], ss1.at[d], rs1.at[d], peers[d])
        c.start()
        sends.append(c)
    acc = block(x_ref, me)[...]
    for d in range(1, n):
        _rcopy("feat", recv.at[srcs[d]], recv.at[srcs[d]], ss1.at[d], rs1.at[d], srcs[d]).wait_recv()
        acc = acc + recv[srcs[d]]
    gath[me] = acc
    sends2 = []
    for d in range(1, n):
        c = _rcopy("feat", gath.at[me], gath.at[me], ss2.at[d], rs2.at[d], peers[d])
        c.start()
        sends2.append(c)
    for c in sends:
        c.wait_send()
    for d in range(1, n):
        _rcopy("feat", gath.at[srcs[d]], gath.at[srcs[d]], ss2.at[d], rs2.at[d], srcs[d]).wait_recv()
    for c in sends2:
        c.wait_send()
    for p in range(n):
        r, c = (p // cblocks) * rh, (p % cblocks) * cw
        o_ref[r:r + rh, c:c + cw] = gath[p]


def _rows_allreduce(nx, x_ref, o_ref, ra, hbuf, rb, rc, gb, ge,
                    ssa, rsa, ssb, rsb, ssc, rsc, ssd, rsd, sse, rse):
    r = lax.axis_index("rows")
    n = 4 * nx
    half, blk = x_ref.shape[0] // 2, x_ref.shape[0] // (2 * nx)
    c = lax.rem(r, 2)
    xi = lax.rem(r // 2, nx)
    base = r - 2 * xi
    partner = r + 1 - 2 * c
    xpeers = [base + 2 * lax.rem(xi + d, nx) for d in range(nx)]
    xsrcs = [lax.rem(xi + nx - d, nx) for d in range(nx)]
    zpeer = lax.rem(r + 2 * nx, n)
    rcopy = functools.partial(_rcopy, "rows")

    mine = pl.multiple_of(c * half, 8)
    other = pl.multiple_of((1 - c) * half, 8)
    a = rcopy(x_ref.at[pl.ds(other, half)], ra, ssa, rsa, partner)
    a.start()
    a.wait()
    hbuf[...] = x_ref[pl.ds(mine, half), :] + ra[...]

    bs = []
    for d in range(1, nx):
        j = lax.rem(xi + d, nx)
        cp = rcopy(hbuf.at[pl.ds(pl.multiple_of(j * blk, 8), blk)], rb.at[xi],
                   ssb.at[d], rsb.at[d], xpeers[d])
        cp.start()
        bs.append(cp)
    acc = hbuf[pl.ds(pl.multiple_of(xi * blk, 8), blk), :]
    for d in range(1, nx):
        rcopy(rb.at[xsrcs[d]], rb.at[xsrcs[d]], ssb.at[d], rsb.at[d], xpeers[d]).wait_recv()
        acc = acc + rb[xsrcs[d]]
    gb[xi] = acc

    cz = rcopy(gb.at[xi], rc, ssc, rsc, zpeer)
    cz.start()
    cz.wait()
    gb[xi] = gb[xi] + rc[...]

    ds_ = []
    for d in range(1, nx):
        cp = rcopy(gb.at[xi], gb.at[xi], ssd.at[d], rsd.at[d], xpeers[d])
        cp.start()
        ds_.append(cp)
    for cp in bs:
        cp.wait_send()
    for d in range(1, nx):
        rcopy(gb.at[xsrcs[d]], gb.at[xsrcs[d]], ssd.at[d], rsd.at[d], xpeers[d]).wait_recv()
    for cp in ds_:
        cp.wait_send()

    e = rcopy(gb, ge, sse, rse, partner)
    e.start()
    e.wait()
    for j in range(nx):
        o_ref[pl.ds(pl.multiple_of(mine + j * blk, 8), blk), :] = gb[j]
        o_ref[pl.ds(pl.multiple_of(other + j * blk, 8), blk), :] = ge[j]


def _fused_kernel(nf, nr, rh, cw, design, lab, x0, dual, cz, eta, rho, lim,
                  ox, oz, ou, pbuf, mbuf, rbuf, sbuf, *scratch):
    feat_scr = scratch[:12]
    rows_scr = scratch[12:]
    nx = nr // 4

    me_f = lax.axis_index("feat")
    r = lax.axis_index("rows")
    fpeers = [lax.rem(me_f + d, nf) for d in range(1, nf)]
    c = lax.rem(r, 2)
    xi = lax.rem(r // 2, nx)
    rpeers = [r + 1 - 2 * c, lax.rem(r + 2 * nx, nr)]
    rpeers += [r - 2 * xi + 2 * lax.rem(xi + d, nx) for d in range(1, nx)]

    barrier = pltpu.get_barrier_semaphore()
    for p in fpeers:
        pl.semaphore_signal(barrier, inc=1, device_id=_device("feat", p), device_id_type=MESH)
    for p in rpeers:
        pl.semaphore_signal(barrier, inc=1, device_id=_device("rows", p), device_id_type=MESH)
    pl.semaphore_wait(barrier, len(fpeers) + len(rpeers))

    ox[...] = x0[...]
    ntile = design.shape[1] // TILE
    for turn in range(2):
        def margin_body(k, acc):
            cols = pl.ds(pl.multiple_of(k * TILE, TILE), TILE)
            xk = ox[:, cols].astype(jnp.bfloat16)
            return acc + lax.dot_general(
                xk, design[:, cols], (((1,), (1,)), ((), ())),
                preferred_element_type=jnp.float32)

        pbuf[...] = lax.fori_loop(0, ntile, margin_body, jnp.zeros(pbuf.shape, jnp.float32))
        _feat_allreduce(nf, rh, cw, pbuf, mbuf, *feat_scr[turn * 6:(turn + 1) * 6])
        sign = lab[...].astype(jnp.float32)
        rbuf[...] = (sign * jax.nn.sigmoid(-sign * mbuf[...])).astype(jnp.bfloat16)

        def grad_body(j, carry):
            cols = pl.ds(pl.multiple_of(j * TILE, TILE), TILE)
            g = jnp.dot(rbuf[...], design[:, cols], preferred_element_type=jnp.float32)
            x = ox[:, cols]
            ox[:, cols] = x - eta[...] * (rho[...] * (x - cz[:, cols] + dual[:, cols]) - g)
            return carry

        lax.fori_loop(0, ntile, grad_body, 0)

    sbuf[...] = ox[...] + dual[...]
    _rows_allreduce(nx, sbuf, oz, *rows_scr)
    mean = oz[...] / nr
    new_z = mean - jnp.clip(mean, -lim[...], lim[...])
    oz[...] = new_z
    ou[...] = dual[...] + ox[...] - new_z


def _fused(n_rows, n_feat, design, labels, x0, dual, cz, eta, rho, lim):
    k, width = x0.shape
    s = design.shape[0]
    rblocks = min(k // 8, n_feat)
    rh, cw = k // rblocks, s * rblocks // n_feat
    nx = n_rows // 4
    half, blk = k // 2, k // (2 * nx)
    f32 = jnp.float32
    dma = pltpu.SemaphoreType.DMA
    feat_scr = []
    for _ in range(2):
        feat_scr += [pltpu.VMEM((n_feat, rh, cw), f32), pltpu.VMEM((n_feat, rh, cw), f32)]
        feat_scr += [dma((n_feat,)) for _ in range(4)]
    rows_scr = [
        pltpu.VMEM((half, width), f32),
        pltpu.VMEM((half, width), f32),
        pltpu.VMEM((nx, blk, width), f32),
        pltpu.VMEM((blk, width), f32),
        pltpu.VMEM((nx, blk, width), f32),
        pltpu.VMEM((nx, blk, width), f32),
        dma(()), dma(()), dma((nx,)), dma((nx,)), dma(()), dma(()),
        dma((nx,)), dma((nx,)), dma(()), dma(()),
    ]
    vmem = pl.BlockSpec(memory_space=pltpu.VMEM)
    out = jax.ShapeDtypeStruct((k, width), f32)
    return pl.pallas_call(
        functools.partial(_fused_kernel, n_feat, n_rows, rh, cw),
        out_shape=(out, out, out),
        in_specs=[vmem] * 8,
        out_specs=(vmem, vmem, vmem),
        scratch_shapes=[
            pltpu.VMEM((k, s), f32),
            pltpu.VMEM((k, s), f32),
            pltpu.VMEM((k, s), jnp.bfloat16),
            pltpu.VMEM((k, width), f32),
        ] + feat_scr + rows_scr,
        compiler_params=pltpu.CompilerParams(
            collective_id=0, has_side_effects=True, vmem_limit_bytes=60 * 1024 * 1024),
    )(design, labels, x0, dual, cz, eta, rho, lim)


def per_device(n_rows, n_feat, design, labels, local_x, dual_u, consensus_z, step_size, rho, penalty):
    eta = step_size[:, None]
    weight = rho[:, None]
    limit = (penalty / (rho * n_rows))[:, None]
    x, new_z, new_u = _fused(n_rows, n_feat, design, labels, local_x[0], dual_u[0],
                             consensus_z, eta, weight, limit)
    return (x[None], new_z, new_u[None])


def solution(mesh):
    in_specs = (
        P("rows", "feat"),
        P(None, "rows"),
        P("rows", None, "feat"),
        P("rows", None, "feat"),
        P(None, "feat"),
        P(),
        P(),
        P(),
    )
    out_specs = (P("rows", None, "feat"), P(None, "feat"), P("rows", None, "feat"))
    fn = functools.partial(per_device, mesh.shape["rows"], mesh.shape["feat"])
    return jax.shard_map(
        fn, mesh=mesh, in_specs=in_specs, out_specs=out_specs, check_vma=False
    )
```

time: 100 us -> 90.1 us (0.901)
  matrix products: 19.8 us -> 0 us
  local copies, waits for them, and re-layouts: 0.02 us -> 10.2 us
  other arithmetic: 3.91 us -> 0.68 us
  Pallas kernels: 75.4 us -> 78.4 us
    dot_general x4 -> x0, matrix products: 19.8 us -> none  [the longest x2 11.3 us: per_device(): grad = jnp.dot(resid, design, preferred_element_type=jnp.float32)]
    unnamed x10 -> x3, local copies, waits for them, and re-layouts: 0.02 us -> 6.81 us
    broadcast_in_dim x0 -> x3, local copies, waits for them, and re-layouts: none -> 3.43 us  [the longest x1 1.36 us: per_device(): weight = rho[:, None]]
    pallas_call x3 -> x1, Pallas kernels: 75.4 us -> 78.4 us  [_fused(): pl.pallas_call(functools.partial(_fused_kernel, n_feat, n_rows, rh, cw),...]
    broadcast_in_dim x1, other arithmetic: 3.19 us -> 0.68 us  [per_device(): limit = (penalty / (rho * n_rows))[:, None]]
where the time goes in v4:
time: 90.1 us; the launch traced here: 89.9 us
  Pallas kernels  78.4 us (87%)
  local copies, waits for them, and re-layouts  10.2 us (11%)
    pallas_call x1, Pallas kernels, _fused(): pl.pallas_call(functools.partial(_fused_kernel, n_feat, n_rows, rh, cw),...  78.4 us
    unnamed x3, local copies, waits for them, and re-layouts  6.81 us

profile of v4, /device:TPU:1, one launch (start us, length us, event | category | flops | bytes accessed | tf_op | source)
XLA Modules:
  0.0 89.9 jit_solution(12547171107839897377)
XLA Ops:
  0.6 0.7 fusion
  1.3 0.7 copy.13.lim
  2.0 1.4 %copy.11.eta = f32[64,1]{1,0:T(8,128)} copy(f32[64,1]{0,1:T(1,128)} %bitcast.12) | data formatting | bytes 512 | tf_op jit(solution)/shard_map/broadcast_in_dim | solution.py:216
  3.4 1.4 %copy.12.rho = f32[64,1]{1,0:T(8,128)} copy(f32[64,1]{0,1:T(1,128)} %bitcast.13) | data formatting | bytes 512 | tf_op jit(solution)/shard_map/broadcast_in_dim | solution.py:217
  4.7 78.4 %shard_map.103 = (f32[64,4096]{1,0:T(8,128)}, f32[64,4096]{1,0:T(8,128)}, f32[64,4096]{1,0:T(8,128)}) custom-call(bf16[768,4096]{1,0:T(8,128)(2,1)} %design.1, s32[64,768]{1,0:T(8,128)} %lab.1, f32[64,4096]{1,0:T(8,128)} %bitcast.8, f32[64,4096]{1,0:T(8,128)} %bitcast.9, f32[64,4096]{1,0:T(8,128)} %cz.1, f32[64,1]{1,0:T(8,128)} %copy.11.eta, ...), custom_call_target="tpu_custom_call" | custom-call | tf_op jit(solution)/shard_map/pallas_call | solution.py:199
  83.1 2.3 %copy.17 = f32[1,64,4096]{2,1,0:T(8,128)} copy(f32[1,64,4096]{2,1,0:T(8,128)} %bitcast.11) | data formatting | bytes 2097152
  85.4 2.3 %copy.18 = f32[64,4096]{1,0:T(8,128)} copy(f32[64,4096]{1,0:T(8,128)} %get-tuple-element.13) | data formatting | bytes 2097152
  87.6 2.3 %copy.19 = f32[1,64,4096]{2,1,0:T(8,128)} copy(f32[1,64,4096]{2,1,0:T(8,128)} %bitcast.10) | data formatting | bytes 2097152

commit v5 on v4

--- a/solution.py
+++ b/solution.py
@@ -118,8 +118,8 @@
         o_ref[pl.ds(pl.multiple_of(other + j * blk, 8), blk), :] = ge[j]
 
 
-def _fused_kernel(nf, nr, rh, cw, design, lab, x0, dual, cz, eta, rho, lim,
-                  ox, oz, ou, pbuf, mbuf, rbuf, sbuf, *scratch):
+def _fused_kernel(nf, nr, rh, cw, design, lab, x0, dual, cz, prm,
+                  ox, ot, pbuf, mbuf, rbuf, sbuf, *scratch):
     feat_scr = scratch[:12]
     rows_scr = scratch[12:]
     nx = nr // 4
@@ -139,6 +139,8 @@
         pl.semaphore_signal(barrier, inc=1, device_id=_device("rows", p), device_id_type=MESH)
     pl.semaphore_wait(barrier, len(fpeers) + len(rpeers))
 
+    eta = prm[:, 0:1]
+    rho = prm[:, 1:2]
     ox[...] = x0[...]
     ntile = design.shape[1] // TILE
     for turn in range(2):
@@ -158,20 +160,25 @@
             cols = pl.ds(pl.multiple_of(j * TILE, TILE), TILE)
             g = jnp.dot(rbuf[...], design[:, cols], preferred_element_type=jnp.float32)
             x = ox[:, cols]
-            ox[:, cols] = x - eta[...] * (rho[...] * (x - cz[:, cols] + dual[:, cols]) - g)
+            ox[:, cols] = x - eta * (rho * (x - cz[:, cols] + dual[:, cols]) - g)
             return carry
 
         lax.fori_loop(0, ntile, grad_body, 0)
 
     sbuf[...] = ox[...] + dual[...]
-    _rows_allreduce(nx, sbuf, oz, *rows_scr)
-    mean = oz[...] / nr
-    new_z = mean - jnp.clip(mean, -lim[...], lim[...])
+    _rows_allreduce(nx, sbuf, ot, *rows_scr)
+
+
+def _final_kernel(nr, x, total, dual, prm, ox, oz, ou):
+    lim = prm[:, 2:3]
+    mean = total[...] / nr
+    new_z = mean - jnp.clip(mean, -lim, lim)
+    ox[...] = x[...]
     oz[...] = new_z
-    ou[...] = dual[...] + ox[...] - new_z
-
-
-def _fused(n_rows, n_feat, design, labels, x0, dual, cz, eta, rho, lim):
+    ou[...] = dual[...] + x[...] - new_z
+
+
+def _fused(n_rows, n_feat, design, labels, x0, dual, cz, prm):
     k, width = x0.shape
     s = design.shape[0]
     rblocks = min(k // 8, n_feat)
@@ -196,11 +203,11 @@
     ]
     vmem = pl.BlockSpec(memory_space=pltpu.VMEM)
     out = jax.ShapeDtypeStruct((k, width), f32)
-    return pl.pallas_call(
+    x, total = pl.pallas_call(
         functools.partial(_fused_kernel, n_feat, n_rows, rh, cw),
-        out_shape=(out, out, out),
-        in_specs=[vmem] * 8,
-        out_specs=(vmem, vmem, vmem),
+        out_shape=(out, out),
+        in_specs=[vmem] * 6,
+        out_specs=(vmem, vmem),
         scratch_shapes=[
             pltpu.VMEM((k, s), f32),
             pltpu.VMEM((k, s), f32),
@@ -209,15 +216,19 @@
         ] + feat_scr + rows_scr,
         compiler_params=pltpu.CompilerParams(
             collective_id=0, has_side_effects=True, vmem_limit_bytes=60 * 1024 * 1024),
-    )(design, labels, x0, dual, cz, eta, rho, lim)
+    )(design, labels, x0, dual, cz, prm)
+    return pl.pallas_call(
+        functools.partial(_final_kernel, n_rows),
+        out_shape=(out, out, out),
+        in_specs=[vmem] * 4,
+        out_specs=(vmem, vmem, vmem),
+    )(x, total, dual, prm)
 
 
 def per_device(n_rows, n_feat, design, labels, local_x, dual_u, consensus_z, step_size, rho, penalty):
-    eta = step_size[:, None]
-    weight = rho[:, None]
-    limit = (penalty / (rho * n_rows))[:, None]
+    prm = jnp.stack([step_size, rho, penalty / (rho * n_rows)], axis=1)
     x, new_z, new_u = _fused(n_rows, n_feat, design, labels, local_x[0], dual_u[0],
-                             consensus_z, eta, weight, limit)
+                             consensus_z, prm)
     return (x[None], new_z, new_u[None])
 
 

time: 90.1 us -> 84.6 us (0.939)
  local copies, waits for them, and re-layouts: 10.2 us -> 0.7 us
  Pallas kernels: 78.4 us -> 81.7 us
    unnamed x3 -> x0, local copies, waits for them, and re-layouts: 6.81 us -> none
    pallas_call x0 -> x1, Pallas kernels: none -> 3.87 us  [_fused(): pl.pallas_call(functools.partial(_final_kernel, n_rows), out_shape=(out,...]
    broadcast_in_dim x3 -> x0, local copies, waits for them, and re-layouts: 3.43 us -> none  [the longest x1 1.36 us: per_device(): weight = rho[:, None]]
    another operation x0 -> x2, other arithmetic: none -> 1.36 us  [per_device(): prm = jnp.stack([step_size, rho, penalty / (rho * n_rows)], axis=1)]
where the time goes in v5:
time: 84.6 us; the launch traced here: 84.4 us
  Pallas kernels  81.7 us (97%)
  other arithmetic  1.36 us (2%)
    pallas_call x1, Pallas kernels, _fused(): pl.pallas_call(functools.partial(_fused_kernel, n_feat, n_rows, rh, cw),...  77.9 us
    pallas_call x1, Pallas kernels, _fused(): pl.pallas_call(functools.partial(_final_kernel, n_rows), out_shape=(out,...  3.87 us

profile of v5, /device:TPU:1, one launch (start us, length us, event | category | flops | bytes accessed | tf_op | source)
XLA Modules:
  0.0 84.4 jit_solution(18318964505123848139)
XLA Ops:
  0.6 0.7 fusion
  1.3 0.7 pad_maximum_fusion
  2.0 0.7 copy.14.prm
  2.7 77.9 %shard_map.103 = (f32[64,4096]{1,0:T(8,128)}, f32[64,4096]{1,0:T(8,128)}) custom-call(bf16[768,4096]{1,0:T(8,128)(2,1)} %design.1, s32[64,768]{1,0:T(8,128)} %lab.1, f32[64,4096]{1,0:T(8,128)} %bitcast.10, f32[64,4096]{1,0:T(8,128)} %bitcast.8, f32[64,4096]{1,0:T(8,128)} %cz.1, f32[64,3]{1,0:T(8,128)} %copy.14.prm), custom_call_target="tpu_custom_call" | custom-call | tf_op jit(solution)/shard_map/pallas_call | solution.py:206
  80.6 3.9 %shard_map.104 = (f32[64,4096]{1,0:T(8,128)}, f32[64,4096]{1,0:T(8,128)}, f32[64,4096]{1,0:T(8,128)}) custom-call(f32[64,4096]{1,0:T(8,128)} %get-tuple-element.8.x, f32[64,4096]{1,0:T(8,128)} %get-tuple-element.9.total, f32[64,4096]{1,0:T(8,128)} %bitcast.9, f32[64,3]{1,0:T(8,128)} %copy.14.prm), custom_call_target="tpu_custom_call" | custom-call | tf_op jit(solution)/shard_map/pallas_call | solution.py:220

commit v6 on v5

--- a/solution.py
+++ b/solution.py
@@ -10,6 +10,7 @@
 MESH = pl.DeviceIdType.MESH
 AXES = ("rows", "feat")
 TILE = 512
+QCH = 4
 
 
 def _device(axis, peer):
@@ -64,6 +65,7 @@
     r = lax.axis_index("rows")
     n = 4 * nx
     half, blk = x_ref.shape[0] // 2, x_ref.shape[0] // (2 * nx)
+    wq = x_ref.shape[1] // QCH
     c = lax.rem(r, 2)
     xi = lax.rem(r // 2, nx)
     base = r - 2 * xi
@@ -72,50 +74,64 @@
     xsrcs = [lax.rem(xi + nx - d, nx) for d in range(nx)]
     zpeer = lax.rem(r + 2 * nx, n)
     rcopy = functools.partial(_rcopy, "rows")
-
     mine = pl.multiple_of(c * half, 8)
     other = pl.multiple_of((1 - c) * half, 8)
-    a = rcopy(x_ref.at[pl.ds(other, half)], ra, ssa, rsa, partner)
-    a.start()
-    a.wait()
-    hbuf[...] = x_ref[pl.ds(mine, half), :] + ra[...]
-
+
+    def cols(q):
+        return pl.ds(q * wq, wq)
+
+    def rows_of(j):
+        return pl.ds(pl.multiple_of(j * blk, 8), blk)
+
+    a = []
+    for q in range(QCH):
+        cp = rcopy(x_ref.at[pl.ds(other, half), cols(q)], ra.at[:, cols(q)], ssa.at[q], rsa.at[q], partner)
+        cp.start()
+        a.append(cp)
     bs = []
-    for d in range(1, nx):
-        j = lax.rem(xi + d, nx)
-        cp = rcopy(hbuf.at[pl.ds(pl.multiple_of(j * blk, 8), blk)], rb.at[xi],
-                   ssb.at[d], rsb.at[d], xpeers[d])
+    for q in range(QCH):
+        a[q].wait()
+        hbuf[:, cols(q)] = x_ref[pl.ds(mine, half), cols(q)] + ra[:, cols(q)]
+        for d in range(1, nx):
+            j = lax.rem(xi + d, nx)
+            cp = rcopy(hbuf.at[rows_of(j), cols(q)], rb.at[xi, :, cols(q)],
+                       ssb.at[q, d], rsb.at[q, d], xpeers[d])
+            cp.start()
+            bs.append(cp)
+    cz = []
+    for q in range(QCH):
+        acc = hbuf[rows_of(xi), cols(q)]
+        for d in range(1, nx):
+            rcopy(rb.at[xsrcs[d], :, cols(q)], rb.at[xsrcs[d], :, cols(q)],
+                  ssb.at[q, d], rsb.at[q, d], xpeers[d]).wait_recv()
+            acc = acc + rb[xsrcs[d], :, cols(q)]
+        gb[xi, :, cols(q)] = acc
+        cp = rcopy(gb.at[xi, :, cols(q)], rc.at[:, cols(q)], ssc.at[q], rsc.at[q], zpeer)
         cp.start()
-        bs.append(cp)
-    acc = hbuf[pl.ds(pl.multiple_of(xi * blk, 8), blk), :]
-    for d in range(1, nx):
-        rcopy(rb.at[xsrcs[d]], rb.at[xsrcs[d]], ssb.at[d], rsb.at[d], xpeers[d]).wait_recv()
-        acc = acc + rb[xsrcs[d]]
-    gb[xi] = acc
-
-    cz = rcopy(gb.at[xi], rc, ssc, rsc, zpeer)
-    cz.start()
-    cz.wait()
-    gb[xi] = gb[xi] + rc[...]
-
+        cz.append(cp)
     ds_ = []
-    for d in range(1, nx):
-        cp = rcopy(gb.at[xi], gb.at[xi], ssd.at[d], rsd.at[d], xpeers[d])
+    for q in range(QCH):
+        cz[q].wait()
+        gb[xi, :, cols(q)] = gb[xi, :, cols(q)] + rc[:, cols(q)]
+        for d in range(1, nx):
+            cp = rcopy(gb.at[xi, :, cols(q)], gb.at[xi, :, cols(q)], ssd.at[q, d], rsd.at[q, d], xpeers[d])
+            cp.start()
+            ds_.append(cp)
+    e = []
+    for q in range(QCH):
+        for d in range(1, nx):
+            rcopy(gb.at[xsrcs[d], :, cols(q)], gb.at[xsrcs[d], :, cols(q)],
+                  ssd.at[q, d], rsd.at[q, d], xpeers[d]).wait_recv()
+        cp = rcopy(gb.at[:, :, cols(q)], ge.at[:, :, cols(q)], sse.at[q], rse.at[q], partner)
         cp.start()
-        ds_.append(cp)
-    for cp in bs:
+        e.append(cp)
+    for cp in bs + ds_:
         cp.wait_send()
-    for d in range(1, nx):
-        rcopy(gb.at[xsrcs[d]], gb.at[xsrcs[d]], ssd.at[d], rsd.at[d], xpeers[d]).wait_recv()
-    for cp in ds_:
-        cp.wait_send()
-
-    e = rcopy(gb, ge, sse, rse, partner)
-    e.start()
-    e.wait()
-    for j in range(nx):
-        o_ref[pl.ds(pl.multiple_of(mine + j * blk, 8), blk), :] = gb[j]
-        o_ref[pl.ds(pl.multiple_of(other + j * blk, 8), blk), :] = ge[j]
+    for q in range(QCH):
+        e[q].wait()
+        for j in range(nx):
+            o_ref[pl.ds(pl.multiple_of(mine + j * blk, 8), blk), cols(q)] = gb[j, :, cols(q)]
+            o_ref[pl.ds(pl.multiple_of(other + j * blk, 8), blk), cols(q)] = ge[j, :, cols(q)]
 
 
 def _fused_kernel(nf, nr, rh, cw, design, lab, x0, dual, cz, prm,
@@ -198,8 +214,8 @@
         pltpu.VMEM((blk, width), f32),
         pltpu.VMEM((nx, blk, width), f32),
         pltpu.VMEM((nx, blk, width), f32),
-        dma(()), dma(()), dma((nx,)), dma((nx,)), dma(()), dma(()),
-        dma((nx,)), dma((nx,)), dma(()), dma(()),
+        dma((QCH,)), dma((QCH,)), dma((QCH, nx)), dma((QCH, nx)), dma((QCH,)), dma((QCH,)),
+        dma((QCH, nx)), dma((QCH, nx)), dma((QCH,)), dma((QCH,)),
     ]
     vmem = pl.BlockSpec(memory_space=pltpu.VMEM)
     out = jax.ShapeDtypeStruct((k, width), f32)

time: 84.6 us -> 78 us (0.922)
  Pallas kernels: 81.7 us -> 75.2 us
    pallas_call x1, Pallas kernels: 77.9 us -> 71.3 us  [_fused(): pl.pallas_call(functools.partial(_fused_kernel, n_feat, n_rows, rh, cw),...]
where the time goes in v6:
time: 78 us; the launch traced here: 77.9 us
  Pallas kernels  75.2 us (96%)
  other arithmetic  1.36 us (2%)
    pallas_call x1, Pallas kernels, _fused(): pl.pallas_call(functools.partial(_fused_kernel, n_feat, n_rows, rh, cw),...  71.3 us
    pallas_call x1, Pallas kernels, _fused(): pl.pallas_call(functools.partial(_final_kernel, n_rows), out_shape=(out,...  3.87 us

profile of v6, /device:TPU:1, one launch (start us, length us, event | category | flops | bytes accessed | tf_op | source)
XLA Modules:
  0.0 77.9 jit_solution(12047960666383853674)
XLA Ops:
  0.6 0.7 fusion
  1.3 0.7 pad_maximum_fusion
  2.0 0.7 copy.14.prm
  2.7 71.3 %shard_map.103 = (f32[64,4096]{1,0:T(8,128)}, f32[64,4096]{1,0:T(8,128)}) custom-call(bf16[768,4096]{1,0:T(8,128)(2,1)} %design.1, s32[64,768]{1,0:T(8,128)} %lab.1, f32[64,4096]{1,0:T(8,128)} %bitcast.10, f32[64,4096]{1,0:T(8,128)} %bitcast.8, f32[64,4096]{1,0:T(8,128)} %cz.1, f32[64,3]{1,0:T(8,128)} %copy.14.prm), custom_call_target="tpu_custom_call" | custom-call | tf_op jit(solution)/shard_map/pallas_call | solution.py:222
  74.0 3.9 %shard_map.104 = (f32[64,4096]{1,0:T(8,128)}, f32[64,4096]{1,0:T(8,128)}, f32[64,4096]{1,0:T(8,128)}) custom-call(f32[64,4096]{1,0:T(8,128)} %get-tuple-element.8.x, f32[64,4096]{1,0:T(8,128)} %get-tuple-element.9.total, f32[64,4096]{1,0:T(8,128)} %bitcast.9, f32[64,3]{1,0:T(8,128)} %copy.14.prm), custom_call_target="tpu_custom_call" | custom-call | tf_op jit(solution)/shard_map/pallas_call | solution.py:236

commit v7 on v6

--- a/solution.py
+++ b/solution.py
@@ -10,7 +10,7 @@
 MESH = pl.DeviceIdType.MESH
 AXES = ("rows", "feat")
 TILE = 512
-QCH = 4
+QCH = 8
 
 
 def _device(axis, peer):
@@ -134,8 +134,12 @@
             o_ref[pl.ds(pl.multiple_of(other + j * blk, 8), blk), cols(q)] = ge[j, :, cols(q)]
 
 
-def _fused_kernel(nf, nr, rh, cw, design, lab, x0, dual, cz, prm,
-                  ox, ot, pbuf, mbuf, rbuf, sbuf, *scratch):
+def _fused_kernel(nf, nr, rh, cw, design_hbm, lab, x0, dual_hbm, cz_hbm, prm,
+                  ox, ot, pbuf, mbuf, rbuf, sbuf, design, dual, cz, lsem, *scratch):
+    loads = [pltpu.make_async_copy(src, dst, lsem.at[i])
+             for i, (src, dst) in enumerate([(design_hbm, design), (dual_hbm, dual), (cz_hbm, cz)])]
+    for cp in loads:
+        cp.start()
     feat_scr = scratch[:12]
     rows_scr = scratch[12:]
     nx = nr // 4
@@ -159,6 +163,7 @@
     rho = prm[:, 1:2]
     ox[...] = x0[...]
     ntile = design.shape[1] // TILE
+    loads[0].wait()
     for turn in range(2):
         def margin_body(k, acc):
             cols = pl.ds(pl.multiple_of(k * TILE, TILE), TILE)
@@ -171,6 +176,9 @@
         _feat_allreduce(nf, rh, cw, pbuf, mbuf, *feat_scr[turn * 6:(turn + 1) * 6])
         sign = lab[...].astype(jnp.float32)
         rbuf[...] = (sign * jax.nn.sigmoid(-sign * mbuf[...])).astype(jnp.bfloat16)
+        if turn == 0:
+            loads[1].wait()
+            loads[2].wait()
 
         def grad_body(j, carry):
             cols = pl.ds(pl.multiple_of(j * TILE, TILE), TILE)
@@ -218,26 +226,33 @@
         dma((QCH, nx)), dma((QCH, nx)), dma((QCH,)), dma((QCH,)),
     ]
     vmem = pl.BlockSpec(memory_space=pltpu.VMEM)
+    hbm = pl.BlockSpec(memory_space=pl.ANY)
     out = jax.ShapeDtypeStruct((k, width), f32)
     x, total = pl.pallas_call(
         functools.partial(_fused_kernel, n_feat, n_rows, rh, cw),
         out_shape=(out, out),
-        in_specs=[vmem] * 6,
+        in_specs=[hbm, vmem, vmem, hbm, hbm, vmem],
         out_specs=(vmem, vmem),
         scratch_shapes=[
             pltpu.VMEM((k, s), f32),
             pltpu.VMEM((k, s), f32),
             pltpu.VMEM((k, s), jnp.bfloat16),
             pltpu.VMEM((k, width), f32),
+            pltpu.VMEM(design.shape, design.dtype),
+            pltpu.VMEM((k, width), f32),
+            pltpu.VMEM((k, width), f32),
+            dma((3,)),
         ] + feat_scr + rows_scr,
         compiler_params=pltpu.CompilerParams(
             collective_id=0, has_side_effects=True, vmem_limit_bytes=60 * 1024 * 1024),
     )(design, labels, x0, dual, cz, prm)
+    tile = pl.BlockSpec((k, 2 * TILE), lambda j: (0, j))
     return pl.pallas_call(
         functools.partial(_final_kernel, n_rows),
         out_shape=(out, out, out),
-        in_specs=[vmem] * 4,
-        out_specs=(vmem, vmem, vmem),
+        grid=(width // (2 * TILE),),
+        in_specs=[tile, tile, tile, pl.BlockSpec(prm.shape, lambda j: (0, 0))],
+        out_specs=(tile, tile, tile),
     )(x, total, dual, prm)
 
 

time: 78 us -> 76.1 us (0.976)
  Pallas kernels: 75.2 us -> 73.1 us
    pallas_call x1, Pallas kernels: 71.3 us -> 69 us  [_fused(): pl.pallas_call(functools.partial(_fused_kernel, n_feat, n_rows, rh, cw),...]
where the time goes in v7:
time: 76.1 us; the launch traced here: 75.9 us
  Pallas kernels  73.1 us (96%)
  other arithmetic  1.36 us (2%)
    pallas_call x1, Pallas kernels, _fused(): pl.pallas_call(functools.partial(_fused_kernel, n_feat, n_rows, rh, cw),...  69 us
    pallas_call x1, Pallas kernels, _fused(): pl.pallas_call(functools.partial(_final_kernel, n_rows), out_shape=(out,...  4.12 us

profile of v7, /device:TPU:1, one launch (start us, length us, event | category | flops | bytes accessed | tf_op | source)
XLA Modules:
  0.0 75.9 jit_solution(7587546238307383382)
XLA Ops:
  0.6 0.7 fusion
  1.3 0.7 pad_maximum_fusion
  2.0 0.7 copy.14.prm
  2.7 69.0 %shard_map.103 = (f32[64,4096]{1,0:T(8,128)}, f32[64,4096]{1,0:T(8,128)}) custom-call(bf16[768,4096]{1,0:T(8,128)(2,1)} %design_hbm.1, s32[64,768]{1,0:T(8,128)} %lab.1, f32[64,4096]{1,0:T(8,128)} %bitcast.10, f32[64,4096]{1,0:T(8,128)} %bitcast.8, f32[64,4096]{1,0:T(8,128)} %cz_hbm.1, f32[64,3]{1,0:T(8,128)} %copy.14.prm), custom_call_target="tpu_custom_call" | custom-call | tf_op jit(solution)/shard_map/pallas_call | solution.py:231
  71.7 4.1 %shard_map.104 = (f32[64,4096]{1,0:T(8,128)}, f32[64,4096]{1,0:T(8,128)}, f32[64,4096]{1,0:T(8,128)}) custom-call(f32[64,4096]{1,0:T(8,128)} %get-tuple-element.8.x, f32[64,4096]{1,0:T(8,128)} %get-tuple-element.9.total, f32[64,4096]{1,0:T(8,128)} %bitcast.9, f32[64,3]{1,0:T(8,128)} %copy.14.prm), custom_call_target="tpu_custom_call" | custom-call | tf_op jit(solution)/shard_map/pallas_call | solution.py:250

commit v8 on v7

--- a/solution.py
+++ b/solution.py
@@ -83,11 +83,8 @@
     def rows_of(j):
         return pl.ds(pl.multiple_of(j * blk, 8), blk)
 
-    a = []
-    for q in range(QCH):
-        cp = rcopy(x_ref.at[pl.ds(other, half), cols(q)], ra.at[:, cols(q)], ssa.at[q], rsa.at[q], partner)
-        cp.start()
-        a.append(cp)
+    a = [rcopy(x_ref.at[pl.ds(other, half), cols(q)], ra.at[:, cols(q)], ssa.at[q], rsa.at[q], partner)
+         for q in range(QCH)]
     bs = []
     for q in range(QCH):
         a[q].wait()
@@ -157,7 +154,6 @@
         pl.semaphore_signal(barrier, inc=1, device_id=_device("feat", p), device_id_type=MESH)
     for p in rpeers:
         pl.semaphore_signal(barrier, inc=1, device_id=_device("rows", p), device_id_type=MESH)
-    pl.semaphore_wait(barrier, len(fpeers) + len(rpeers))
 
     eta = prm[:, 0:1]
     rho = prm[:, 1:2]
@@ -173,6 +169,8 @@
                 preferred_element_type=jnp.float32)
 
         pbuf[...] = lax.fori_loop(0, ntile, margin_body, jnp.zeros(pbuf.shape, jnp.float32))
+        if turn == 0:
+            pl.semaphore_wait(barrier, len(fpeers) + len(rpeers))
         _feat_allreduce(nf, rh, cw, pbuf, mbuf, *feat_scr[turn * 6:(turn + 1) * 6])
         sign = lab[...].astype(jnp.float32)
         rbuf[...] = (sign * jax.nn.sigmoid(-sign * mbuf[...])).astype(jnp.bfloat16)
@@ -184,12 +182,18 @@
             cols = pl.ds(pl.multiple_of(j * TILE, TILE), TILE)
             g = jnp.dot(rbuf[...], design[:, cols], preferred_element_type=jnp.float32)
             x = ox[:, cols]
-            ox[:, cols] = x - eta * (rho * (x - cz[:, cols] + dual[:, cols]) - g)
+            x = x - eta * (rho * (x - cz[:, cols] + dual[:, cols]) - g)
+            ox[:, cols] = x
+            if turn == 1:
+                sbuf[:, cols] = x + dual[:, cols]
+                half = x.shape[0] // 2
+                other = pl.multiple_of((1 - lax.rem(r, 2)) * half, 8)
+                _rcopy("rows", sbuf.at[pl.ds(other, half), cols], rows_scr[0].at[:, cols],
+                       rows_scr[6].at[j], rows_scr[7].at[j], rpeers[0]).start()
             return carry
 
         lax.fori_loop(0, ntile, grad_body, 0)
 
-    sbuf[...] = ox[...] + dual[...]
     _rows_allreduce(nx, sbuf, ot, *rows_scr)
 
 

time: 76.1 us -> 74 us (0.972)
  Pallas kernels: 73.1 us -> 71.1 us
    pallas_call x1, Pallas kernels: 69 us -> 67 us  [_fused(): pl.pallas_call(functools.partial(_fused_kernel, n_feat, n_rows, rh, cw),...]
where the time goes in v8:
time: 74 us; the launch traced here: 73.8 us
  Pallas kernels  71.1 us (96%)
  other arithmetic  1.36 us (2%)
    pallas_call x1, Pallas kernels, _fused(): pl.pallas_call(functools.partial(_fused_kernel, n_feat, n_rows, rh, cw),...  67 us
    pallas_call x1, Pallas kernels, _fused(): pl.pallas_call(functools.partial(_final_kernel, n_rows), out_shape=(out,...  4.12 us

profile of v8, /device:TPU:1, one launch (start us, length us, event | category | flops | bytes accessed | tf_op | source)
XLA Modules:
  0.0 73.8 jit_solution(11345654813581827957)
XLA Ops:
  0.6 0.7 fusion
  1.3 0.7 pad_maximum_fusion
  2.0 0.7 copy.14.prm
  2.7 67.0 %shard_map.103 = (f32[64,4096]{1,0:T(8,128)}, f32[64,4096]{1,0:T(8,128)}) custom-call(bf16[768,4096]{1,0:T(8,128)(2,1)} %design_hbm.1, s32[64,768]{1,0:T(8,128)} %lab.1, f32[64,4096]{1,0:T(8,128)} %bitcast.10, f32[64,4096]{1,0:T(8,128)} %bitcast.8, f32[64,4096]{1,0:T(8,128)} %cz_hbm.1, f32[64,3]{1,0:T(8,128)} %copy.14.prm), custom_call_target="tpu_custom_call" | custom-call | tf_op jit(solution)/shard_map/pallas_call | solution.py:235
  69.7 4.1 %shard_map.104 = (f32[64,4096]{1,0:T(8,128)}, f32[64,4096]{1,0:T(8,128)}, f32[64,4096]{1,0:T(8,128)}) custom-call(f32[64,4096]{1,0:T(8,128)} %get-tuple-element.8.x, f32[64,4096]{1,0:T(8,128)} %get-tuple-element.9.total, f32[64,4096]{1,0:T(8,128)} %bitcast.9, f32[64,3]{1,0:T(8,128)} %copy.14.prm), custom_call_target="tpu_custom_call" | custom-call | tf_op jit(solution)/shard_map/pallas_call | solution.py:254

commit v9 on v8

--- a/solution.py
+++ b/solution.py
@@ -23,25 +23,30 @@
         device_id=_device(axis, p), device_id_type=MESH)
 
 
-def _feat_allreduce(n, rh, cw, x_ref, o_ref, recv, gath, ss1, rs1, ss2, rs2):
+def _feat_block(rh, cw, cblocks, ref, p):
+    r = pl.multiple_of((p // cblocks) * rh, 8)
+    c = pl.multiple_of((p % cblocks) * cw, 128)
+    return ref.at[pl.ds(r, rh), pl.ds(c, cw)]
+
+
+def _feat_send(n, rh, cw, x_ref, recv, ss1, rs1, h):
+    me = lax.axis_index("feat")
+    cblocks = x_ref.shape[1] // cw
+    for p in range(h, n, cblocks):
+        @pl.when(me != p)
+        def _():
+            _rcopy("feat", _feat_block(rh, cw, cblocks, x_ref, p), recv.at[me],
+                   ss1.at[p], rs1.at[me], p).start()
+
+
+def _feat_finish(n, rh, cw, x_ref, o_ref, recv, gath, ss1, rs1, ss2, rs2):
     me = lax.axis_index("feat")
     peers = [lax.rem(me + d, n) for d in range(n)]
     srcs = [lax.rem(me + n - d, n) for d in range(n)]
     cblocks = x_ref.shape[1] // cw
-
-    def block(ref, p):
-        r = pl.multiple_of((p // cblocks) * rh, 8)
-        c = pl.multiple_of((p % cblocks) * cw, 128)
-        return ref.at[pl.ds(r, rh), pl.ds(c, cw)]
-
-    sends = []
+    acc = _feat_block(rh, cw, cblocks, x_ref, me)[...]
     for d in range(1, n):
-        c = _rcopy("feat", block(x_ref, peers[d]), recv.at[me], ss1.at[d], rs1.at[d], peers[d])
-        c.start()
-        sends.append(c)
-    acc = block(x_ref, me)[...]
-    for d in range(1, n):
-        _rcopy("feat", recv.at[srcs[d]], recv.at[srcs[d]], ss1.at[d], rs1.at[d], srcs[d]).wait_recv()
+        _rcopy("feat", recv.at[srcs[d]], recv.at[srcs[d]], ss1.at[0], rs1.at[srcs[d]], srcs[d]).wait_recv()
         acc = acc + recv[srcs[d]]
     gath[me] = acc
     sends2 = []
@@ -49,8 +54,11 @@
         c = _rcopy("feat", gath.at[me], gath.at[me], ss2.at[d], rs2.at[d], peers[d])
         c.start()
         sends2.append(c)
-    for c in sends:
-        c.wait_send()
+    for p in range(n):
+        @pl.when(me != p)
+        def _():
+            _rcopy("feat", _feat_block(rh, cw, cblocks, x_ref, p), recv.at[me],
+                   ss1.at[p], rs1.at[me], p).wait_send()
     for d in range(1, n):
         _rcopy("feat", gath.at[srcs[d]], gath.at[srcs[d]], ss2.at[d], rs2.at[d], srcs[d]).wait_recv()
     for c in sends2:
@@ -159,19 +167,25 @@
     rho = prm[:, 1:2]
     ox[...] = x0[...]
     ntile = design.shape[1] // TILE
+    cblocks = design.shape[0] // cw
     loads[0].wait()
     for turn in range(2):
-        def margin_body(k, acc):
+        def margin_body(sc, k, acc):
             cols = pl.ds(pl.multiple_of(k * TILE, TILE), TILE)
             xk = ox[:, cols].astype(jnp.bfloat16)
             return acc + lax.dot_general(
-                xk, design[:, cols], (((1,), (1,)), ((), ())),
+                xk, design[sc, cols], (((1,), (1,)), ((), ())),
                 preferred_element_type=jnp.float32)
 
-        pbuf[...] = lax.fori_loop(0, ntile, margin_body, jnp.zeros(pbuf.shape, jnp.float32))
-        if turn == 0:
-            pl.semaphore_wait(barrier, len(fpeers) + len(rpeers))
-        _feat_allreduce(nf, rh, cw, pbuf, mbuf, *feat_scr[turn * 6:(turn + 1) * 6])
+        fs = feat_scr[turn * 6:(turn + 1) * 6]
+        for h in range(cblocks):
+            sc = pl.ds(h * cw, cw)
+            pbuf[:, sc] = lax.fori_loop(
+                0, ntile, functools.partial(margin_body, sc), jnp.zeros((pbuf.shape[0], cw), jnp.float32))
+            if turn == 0 and h == 0:
+                pl.semaphore_wait(barrier, len(fpeers) + len(rpeers))
+            _feat_send(nf, rh, cw, pbuf, fs[0], fs[2], fs[3], h)
+        _feat_finish(nf, rh, cw, pbuf, mbuf, *fs)
         sign = lab[...].astype(jnp.float32)
         rbuf[...] = (sign * jax.nn.sigmoid(-sign * mbuf[...])).astype(jnp.bfloat16)
         if turn == 0:

time: 74 us -> 75.7 us (1.023)
  Pallas kernels: 71.1 us -> 72.8 us
    pallas_call x1, Pallas kernels: 67 us -> 68.7 us  [_fused(): pl.pallas_call(functools.partial(_fused_kernel, n_feat, n_rows, rh, cw),...]
where the time goes in v9:
time: 75.7 us; the launch traced here: 75.5 us
  Pallas kernels  72.8 us (96%)
  other arithmetic  1.36 us (2%)
    pallas_call x1, Pallas kernels, _fused(): pl.pallas_call(functools.partial(_fused_kernel, n_feat, n_rows, rh, cw),...  68.7 us
    pallas_call x1, Pallas kernels, _fused(): pl.pallas_call(functools.partial(_final_kernel, n_rows), out_shape=(out,...  4.12 us

profile of v9, /device:TPU:1, one launch (start us, length us, event | category | flops | bytes accessed | tf_op | source)
XLA Modules:
  0.0 75.5 jit_solution(4444231499253322909)
XLA Ops:
  0.6 0.7 fusion
  1.3 0.7 pad_maximum_fusion
  2.0 0.7 copy.14.prm
  2.7 68.7 %shard_map.103 = (f32[64,4096]{1,0:T(8,128)}, f32[64,4096]{1,0:T(8,128)}) custom-call(bf16[768,4096]{1,0:T(8,128)(2,1)} %design_hbm.1, s32[64,768]{1,0:T(8,128)} %lab.1, f32[64,4096]{1,0:T(8,128)} %bitcast.10, f32[64,4096]{1,0:T(8,128)} %bitcast.8, f32[64,4096]{1,0:T(8,128)} %cz_hbm.1, f32[64,3]{1,0:T(8,128)} %copy.14.prm), custom_call_target="tpu_custom_call" | custom-call | tf_op jit(solution)/shard_map/pallas_call | solution.py:249
  71.4 4.1 %shard_map.104 = (f32[64,4096]{1,0:T(8,128)}, f32[64,4096]{1,0:T(8,128)}, f32[64,4096]{1,0:T(8,128)}) custom-call(f32[64,4096]{1,0:T(8,128)} %get-tuple-element.8.x, f32[64,4096]{1,0:T(8,128)} %get-tuple-element.9.total, f32[64,4096]{1,0:T(8,128)} %bitcast.9, f32[64,3]{1,0:T(8,128)} %copy.14.prm), custom_call_target="tpu_custom_call" | custom-call | tf_op jit(solution)/shard_map/pallas_call | solution.py:268

commit v10 on v8

--- a/solution.py
+++ b/solution.py
@@ -168,7 +168,8 @@
                 xk, design[:, cols], (((1,), (1,)), ((), ())),
                 preferred_element_type=jnp.float32)
 
-        pbuf[...] = lax.fori_loop(0, ntile, margin_body, jnp.zeros(pbuf.shape, jnp.float32))
+        if turn == 0:
+            pbuf[...] = lax.fori_loop(0, ntile, margin_body, jnp.zeros(pbuf.shape, jnp.float32))
         if turn == 0:
             pl.semaphore_wait(barrier, len(fpeers) + len(rpeers))
         _feat_allreduce(nf, rh, cw, pbuf, mbuf, *feat_scr[turn * 6:(turn + 1) * 6])
@@ -184,15 +185,23 @@
             x = ox[:, cols]
             x = x - eta * (rho * (x - cz[:, cols] + dual[:, cols]) - g)
             ox[:, cols] = x
+            if turn == 0:
+                nxt = carry + lax.dot_general(
+                    x.astype(jnp.bfloat16), design[:, cols], (((1,), (1,)), ((), ())),
+                    preferred_element_type=jnp.float32)
             if turn == 1:
                 sbuf[:, cols] = x + dual[:, cols]
                 half = x.shape[0] // 2
                 other = pl.multiple_of((1 - lax.rem(r, 2)) * half, 8)
                 _rcopy("rows", sbuf.at[pl.ds(other, half), cols], rows_scr[0].at[:, cols],
                        rows_scr[6].at[j], rows_scr[7].at[j], rpeers[0]).start()
-            return carry
-
-        lax.fori_loop(0, ntile, grad_body, 0)
+                nxt = carry
+            return nxt
+
+        if turn == 0:
+            pbuf[...] = lax.fori_loop(0, ntile, grad_body, jnp.zeros(pbuf.shape, jnp.float32))
+        else:
+            lax.fori_loop(0, ntile, grad_body, 0)
 
     _rows_allreduce(nx, sbuf, ot, *rows_scr)
 

time: 74 us -> 73.4 us (level)
  no operation moved by 1% of the time
where the time goes in v10:
time: 73.4 us; the launch traced here: 73.2 us
  Pallas kernels  70.5 us (96%)
  other arithmetic  1.36 us (2%)
    pallas_call x1, Pallas kernels, _fused(): pl.pallas_call(functools.partial(_fused_kernel, n_feat, n_rows, rh, cw),...  66.4 us
    pallas_call x1, Pallas kernels, _fused(): pl.pallas_call(functools.partial(_final_kernel, n_rows), out_shape=(out,...  4.12 us

profile of v10, /device:TPU:1, one launch (start us, length us, event | category | flops | bytes accessed | tf_op | source)
XLA Modules:
  0.0 73.2 jit_solution(16688969723751296075)
XLA Ops:
  0.6 0.7 fusion
  1.3 0.7 pad_maximum_fusion
  2.0 0.7 copy.14.prm
  2.7 66.4 %shard_map.103 = (f32[64,4096]{1,0:T(8,128)}, f32[64,4096]{1,0:T(8,128)}) custom-call(bf16[768,4096]{1,0:T(8,128)(2,1)} %design_hbm.1, s32[64,768]{1,0:T(8,128)} %lab.1, f32[64,4096]{1,0:T(8,128)} %bitcast.10, f32[64,4096]{1,0:T(8,128)} %bitcast.8, f32[64,4096]{1,0:T(8,128)} %cz_hbm.1, f32[64,3]{1,0:T(8,128)} %copy.14.prm), custom_call_target="tpu_custom_call" | custom-call | tf_op jit(solution)/shard_map/pallas_call | solution.py:244
  69.1 4.1 %shard_map.104 = (f32[64,4096]{1,0:T(8,128)}, f32[64,4096]{1,0:T(8,128)}, f32[64,4096]{1,0:T(8,128)}) custom-call(f32[64,4096]{1,0:T(8,128)} %get-tuple-element.8.x, f32[64,4096]{1,0:T(8,128)} %get-tuple-element.9.total, f32[64,4096]{1,0:T(8,128)} %bitcast.9, f32[64,3]{1,0:T(8,128)} %copy.14.prm), custom_call_target="tpu_custom_call" | custom-call | tf_op jit(solution)/shard_map/pallas_call | solution.py:263

commit v11 on v10

--- a/solution.py
+++ b/solution.py
@@ -9,8 +9,8 @@
 
 MESH = pl.DeviceIdType.MESH
 AXES = ("rows", "feat")
-TILE = 512
-QCH = 8
+TILE = 1024
+QCH = 4
 
 
 def _device(axis, peer):

time: 73.4 us -> 71.8 us (0.978)
  Pallas kernels: 70.5 us -> 69 us
    pallas_call x1, Pallas kernels: 4.12 us -> 3.37 us  [_fused(): pl.pallas_call(functools.partial(_final_kernel, n_rows), out_shape=(out,...]
    pallas_call x1, Pallas kernels: 66.4 us -> 65.6 us  [_fused(): pl.pallas_call(functools.partial(_fused_kernel, n_feat, n_rows, rh, cw),...]
where the time goes in v11:
time: 71.8 us; the launch traced here: 71.7 us
  Pallas kernels  69 us (96%)
  other arithmetic  1.36 us (2%)
    pallas_call x1, Pallas kernels, _fused(): pl.pallas_call(functools.partial(_fused_kernel, n_feat, n_rows, rh, cw),...  65.6 us
    pallas_call x1, Pallas kernels, _fused(): pl.pallas_call(functools.partial(_final_kernel, n_rows), out_shape=(out,...  3.37 us

profile of v11, /device:TPU:1, one launch (start us, length us, event | category | flops | bytes accessed | tf_op | source)
XLA Modules:
  0.0 71.7 jit_solution(13598879870221377104)
XLA Ops:
  0.6 0.7 fusion
  1.3 0.7 pad_maximum_fusion
  2.0 0.7 copy.14.prm
  2.7 65.6 %shard_map.103 = (f32[64,4096]{1,0:T(8,128)}, f32[64,4096]{1,0:T(8,128)}) custom-call(bf16[768,4096]{1,0:T(8,128)(2,1)} %design_hbm.1, s32[64,768]{1,0:T(8,128)} %lab.1, f32[64,4096]{1,0:T(8,128)} %bitcast.10, f32[64,4096]{1,0:T(8,128)} %bitcast.8, f32[64,4096]{1,0:T(8,128)} %cz_hbm.1, f32[64,3]{1,0:T(8,128)} %copy.14.prm), custom_call_target="tpu_custom_call" | custom-call | tf_op jit(solution)/shard_map/pallas_call | solution.py:244
  68.3 3.4 %shard_map.104 = (f32[64,4096]{1,0:T(8,128)}, f32[64,4096]{1,0:T(8,128)}, f32[64,4096]{1,0:T(8,128)}) custom-call(f32[64,4096]{1,0:T(8,128)} %get-tuple-element.8.x, f32[64,4096]{1,0:T(8,128)} %get-tuple-element.9.total, f32[64,4096]{1,0:T(8,128)} %bitcast.9, f32[64,3]{1,0:T(8,128)} %copy.14.prm), custom_call_target="tpu_custom_call" | custom-call | tf_op jit(solution)/shard_map/pallas_call | solution.py:263

commit v12 on v11

--- a/solution.py
+++ b/solution.py
@@ -259,11 +259,11 @@
         compiler_params=pltpu.CompilerParams(
             collective_id=0, has_side_effects=True, vmem_limit_bytes=60 * 1024 * 1024),
     )(design, labels, x0, dual, cz, prm)
-    tile = pl.BlockSpec((k, 2 * TILE), lambda j: (0, j))
+    tile = pl.BlockSpec((k, 1024), lambda j: (0, j))
     return pl.pallas_call(
         functools.partial(_final_kernel, n_rows),
         out_shape=(out, out, out),
-        grid=(width // (2 * TILE),),
+        grid=(width // (1024),),
         in_specs=[tile, tile, tile, pl.BlockSpec(prm.shape, lambda j: (0, 0))],
         out_specs=(tile, tile, tile),
     )(x, total, dual, prm)

time: 71.8 us -> 72.7 us (1.013)
    pallas_call x1, Pallas kernels: 3.37 us -> 4.12 us  [_fused(): pl.pallas_call(functools.partial(_final_kernel, n_rows), out_shape=(out,...]
where the time goes in v12:
time: 72.7 us; the launch traced here: 72.5 us
  Pallas kernels  69.7 us (96%)
  other arithmetic  1.36 us (2%)
    pallas_call x1, Pallas kernels, _fused(): pl.pallas_call(functools.partial(_fused_kernel, n_feat, n_rows, rh, cw),...  65.6 us
    pallas_call x1, Pallas kernels, _fused(): pl.pallas_call(functools.partial(_final_kernel, n_rows), out_shape=(out,...  4.12 us

profile of v12, /device:TPU:1, one launch (start us, length us, event | category | flops | bytes accessed | tf_op | source)
XLA Modules:
  0.0 72.5 jit_solution(4686023737201286145)
XLA Ops:
  0.6 0.7 fusion
  1.3 0.7 pad_maximum_fusion
  2.0 0.7 copy.14.prm
  2.7 65.6 %shard_map.103 = (f32[64,4096]{1,0:T(8,128)}, f32[64,4096]{1,0:T(8,128)}) custom-call(bf16[768,4096]{1,0:T(8,128)(2,1)} %design_hbm.1, s32[64,768]{1,0:T(8,128)} %lab.1, f32[64,4096]{1,0:T(8,128)} %bitcast.10, f32[64,4096]{1,0:T(8,128)} %bitcast.8, f32[64,4096]{1,0:T(8,128)} %cz_hbm.1, f32[64,3]{1,0:T(8,128)} %copy.14.prm), custom_call_target="tpu_custom_call" | custom-call | tf_op jit(solution)/shard_map/pallas_call | solution.py:244
  68.3 4.1 %shard_map.104 = (f32[64,4096]{1,0:T(8,128)}, f32[64,4096]{1,0:T(8,128)}, f32[64,4096]{1,0:T(8,128)}) custom-call(f32[64,4096]{1,0:T(8,128)} %get-tuple-element.8.x, f32[64,4096]{1,0:T(8,128)} %get-tuple-element.9.total, f32[64,4096]{1,0:T(8,128)} %bitcast.9, f32[64,3]{1,0:T(8,128)} %copy.14.prm), custom_call_target="tpu_custom_call" | custom-call | tf_op jit(solution)/shard_map/pallas_call | solution.py:263

commit v13 on v11

--- a/solution.py
+++ b/solution.py
@@ -169,7 +169,7 @@
                 preferred_element_type=jnp.float32)
 
         if turn == 0:
-            pbuf[...] = lax.fori_loop(0, ntile, margin_body, jnp.zeros(pbuf.shape, jnp.float32))
+            pbuf[...] = lax.fori_loop(0, ntile, margin_body, jnp.zeros(pbuf.shape, jnp.float32), unroll=True)
         if turn == 0:
             pl.semaphore_wait(barrier, len(fpeers) + len(rpeers))
         _feat_allreduce(nf, rh, cw, pbuf, mbuf, *feat_scr[turn * 6:(turn + 1) * 6])
@@ -199,9 +199,9 @@
             return nxt
 
         if turn == 0:
-            pbuf[...] = lax.fori_loop(0, ntile, grad_body, jnp.zeros(pbuf.shape, jnp.float32))
+            pbuf[...] = lax.fori_loop(0, ntile, grad_body, jnp.zeros(pbuf.shape, jnp.float32), unroll=True)
         else:
-            lax.fori_loop(0, ntile, grad_body, 0)
+            lax.fori_loop(0, ntile, grad_body, 0, unroll=True)
 
     _rows_allreduce(nx, sbuf, ot, *rows_scr)
 

time: 71.8 us -> 71.3 us (level)
  no operation moved by 1% of the time
where the time goes in v13:
time: 71.3 us; the launch traced here: 71.2 us
  Pallas kernels  68.5 us (96%)
  other arithmetic  1.36 us (2%)
    pallas_call x1, Pallas kernels, _fused(): pl.pallas_call(functools.partial(_fused_kernel, n_feat, n_rows, rh, cw),...  65.1 us
    pallas_call x1, Pallas kernels, _fused(): pl.pallas_call(functools.partial(_final_kernel, n_rows), out_shape=(out,...  3.37 us

profile of v13, /device:TPU:1, one launch (start us, length us, event | category | flops | bytes accessed | tf_op | source)
XLA Modules:
  0.0 71.2 jit_solution(11651815411678290412)
XLA Ops:
  0.6 0.7 fusion
  1.3 0.7 pad_maximum_fusion
  2.0 0.7 copy.14.prm
  2.7 65.1 %shard_map.103 = (f32[64,4096]{1,0:T(8,128)}, f32[64,4096]{1,0:T(8,128)}) custom-call(bf16[768,4096]{1,0:T(8,128)(2,1)} %design_hbm.1, s32[64,768]{1,0:T(8,128)} %lab.1, f32[64,4096]{1,0:T(8,128)} %bitcast.10, f32[64,4096]{1,0:T(8,128)} %bitcast.8, f32[64,4096]{1,0:T(8,128)} %cz_hbm.1, f32[64,3]{1,0:T(8,128)} %copy.14.prm), custom_call_target="tpu_custom_call" | custom-call | tf_op jit(solution)/shard_map/pallas_call | solution.py:244
  67.8 3.4 %shard_map.104 = (f32[64,4096]{1,0:T(8,128)}, f32[64,4096]{1,0:T(8,128)}, f32[64,4096]{1,0:T(8,128)}) custom-call(f32[64,4096]{1,0:T(8,128)} %get-tuple-element.8.x, f32[64,4096]{1,0:T(8,128)} %get-tuple-element.9.total, f32[64,4096]{1,0:T(8,128)} %bitcast.9, f32[64,3]{1,0:T(8,128)} %copy.14.prm), custom_call_target="tpu_custom_call" | custom-call | tf_op jit(solution)/shard_map/pallas_call | solution.py:263

commit v14 on v13

--- a/solution.py
+++ b/solution.py
@@ -10,7 +10,7 @@
 MESH = pl.DeviceIdType.MESH
 AXES = ("rows", "feat")
 TILE = 1024
-QCH = 4
+QCH = 8
 
 
 def _device(axis, peer):
@@ -193,8 +193,13 @@
                 sbuf[:, cols] = x + dual[:, cols]
                 half = x.shape[0] // 2
                 other = pl.multiple_of((1 - lax.rem(r, 2)) * half, 8)
-                _rcopy("rows", sbuf.at[pl.ds(other, half), cols], rows_scr[0].at[:, cols],
-                       rows_scr[6].at[j], rows_scr[7].at[j], rpeers[0]).start()
+                per = QCH // ntile
+                wq = sbuf.shape[1] // QCH
+                for h in range(per):
+                    q = j * per + h
+                    cq = pl.ds(pl.multiple_of(q * wq, 128), wq)
+                    _rcopy("rows", sbuf.at[pl.ds(other, half), cq], rows_scr[0].at[:, cq],
+                           rows_scr[6].at[q], rows_scr[7].at[q], rpeers[0]).start()
                 nxt = carry
             return nxt
 

time: 71.3 us -> 70.8 us (level)
  no operation moved by 1% of the time
where the time goes in v14:
time: 70.8 us; the launch traced here: 70.7 us
  Pallas kernels  68 us (96%)
  other arithmetic  1.36 us (2%)
    pallas_call x1, Pallas kernels, _fused(): pl.pallas_call(functools.partial(_fused_kernel, n_feat, n_rows, rh, cw),...  64.6 us
    pallas_call x1, Pallas kernels, _fused(): pl.pallas_call(functools.partial(_final_kernel, n_rows), out_shape=(out,...  3.37 us

profile of v14, /device:TPU:1, one launch (start us, length us, event | category | flops | bytes accessed | tf_op | source)
XLA Modules:
  0.0 70.7 jit_solution(2313478230326199850)
XLA Ops:
  0.6 0.7 fusion
  1.3 0.7 pad_maximum_fusion
  2.0 0.7 copy.14.prm
  2.7 64.6 %shard_map.103 = (f32[64,4096]{1,0:T(8,128)}, f32[64,4096]{1,0:T(8,128)}) custom-call(bf16[768,4096]{1,0:T(8,128)(2,1)} %design_hbm.1, s32[64,768]{1,0:T(8,128)} %lab.1, f32[64,4096]{1,0:T(8,128)} %bitcast.10, f32[64,4096]{1,0:T(8,128)} %bitcast.8, f32[64,4096]{1,0:T(8,128)} %cz_hbm.1, f32[64,3]{1,0:T(8,128)} %copy.14.prm), custom_call_target="tpu_custom_call" | custom-call | tf_op jit(solution)/shard_map/pallas_call | solution.py:249
  67.3 3.4 %shard_map.104 = (f32[64,4096]{1,0:T(8,128)}, f32[64,4096]{1,0:T(8,128)}, f32[64,4096]{1,0:T(8,128)}) custom-call(f32[64,4096]{1,0:T(8,128)} %get-tuple-element.8.x, f32[64,4096]{1,0:T(8,128)} %get-tuple-element.9.total, f32[64,4096]{1,0:T(8,128)} %bitcast.9, f32[64,3]{1,0:T(8,128)} %copy.14.prm), custom_call_target="tpu_custom_call" | custom-call | tf_op jit(solution)/shard_map/pallas_call | solution.py:268

commit v15 on v14

--- a/solution.py
+++ b/solution.py
@@ -10,7 +10,7 @@
 MESH = pl.DeviceIdType.MESH
 AXES = ("rows", "feat")
 TILE = 1024
-QCH = 8
+QCH = 16
 
 
 def _device(axis, peer):

time: 70.8 us -> 72 us (1.017)
  Pallas kernels: 68 us -> 69.2 us
    pallas_call x1, Pallas kernels: 64.6 us -> 65.8 us  [_fused(): pl.pallas_call(functools.partial(_fused_kernel, n_feat, n_rows, rh, cw),...]
where the time goes in v15:
time: 72 us; the launch traced here: 71.9 us
  Pallas kernels  69.2 us (96%)
  other arithmetic  1.36 us (2%)
    pallas_call x1, Pallas kernels, _fused(): pl.pallas_call(functools.partial(_fused_kernel, n_feat, n_rows, rh, cw),...  65.8 us
    pallas_call x1, Pallas kernels, _fused(): pl.pallas_call(functools.partial(_final_kernel, n_rows), out_shape=(out,...  3.37 us

profile of v15, /device:TPU:1, one launch (start us, length us, event | category | flops | bytes accessed | tf_op | source)
XLA Modules:
  0.0 71.9 jit_solution(2464746596280182802)
XLA Ops:
  0.6 0.7 fusion
  1.3 0.7 pad_maximum_fusion
  2.0 0.7 copy.14.prm
  2.7 65.8 %shard_map.103 = (f32[64,4096]{1,0:T(8,128)}, f32[64,4096]{1,0:T(8,128)}) custom-call(bf16[768,4096]{1,0:T(8,128)(2,1)} %design_hbm.1, s32[64,768]{1,0:T(8,128)} %lab.1, f32[64,4096]{1,0:T(8,128)} %bitcast.10, f32[64,4096]{1,0:T(8,128)} %bitcast.8, f32[64,4096]{1,0:T(8,128)} %cz_hbm.1, f32[64,3]{1,0:T(8,128)} %copy.14.prm), custom_call_target="tpu_custom_call" | custom-call | tf_op jit(solution)/shard_map/pallas_call | solution.py:249
  68.5 3.4 %shard_map.104 = (f32[64,4096]{1,0:T(8,128)}, f32[64,4096]{1,0:T(8,128)}, f32[64,4096]{1,0:T(8,128)}) custom-call(f32[64,4096]{1,0:T(8,128)} %get-tuple-element.8.x, f32[64,4096]{1,0:T(8,128)} %get-tuple-element.9.total, f32[64,4096]{1,0:T(8,128)} %bitcast.9, f32[64,3]{1,0:T(8,128)} %copy.14.prm), custom_call_target="tpu_custom_call" | custom-call | tf_op jit(solution)/shard_map/pallas_call | solution.py:268
